TPU v7x, 256 devices: a whole 4x4x8 slice. The times are simulated.
256 devices in a mesh: seq: 32 (over z, x), tp: 8 (over y, core).
Axes of the slice: x: 4, y: 4, z: 8, core: 2. Of those that a mesh axis runs over, the one named last changes fastest.
Arguments:
- tokens_in: bfloat16 [8, 4, 2560], P(None, None, 'tp'), may hold values from -32 to 32
- attn_gain: bfloat16 [2560], replicated, may hold values from 0.25 to 1.75
- mlp_gain: bfloat16 [2560], replicated, may hold values from 0.25 to 1.75
- proj_query: bfloat16 [2560, 2560], P(None, 'tp'), may hold values from -0.125 to 0.125
- proj_key: bfloat16 [2560, 640], P(None, 'tp'), may hold values from -0.125 to 0.125
- proj_value: bfloat16 [2560, 640], P(None, 'tp'), may hold values from -0.125 to 0.125
- proj_out: bfloat16 [2560, 2560], P('tp'), may hold values from -0.125 to 0.125
- proj_gate: bfloat16 [2560, 3456], P(None, 'tp'), may hold values from -0.125 to 0.125
- proj_up: bfloat16 [2560, 3456], P(None, 'tp'), may hold values from -0.125 to 0.125
- proj_down: bfloat16 [3456, 2560], P('tp'), may hold values from -0.109375 to 0.109375
- long_keys: bfloat16 [4096, 8, 80], P('seq', 'tp'), may hold values from -340 to 340
- long_values: bfloat16 [4096, 8, 80], P('seq', 'tp'), may hold values from -6 to 6
- short_keys: bfloat16 [512, 8, 240], P('seq', 'tp'), may hold values from -340 to 340
- short_values: bfloat16 [512, 8, 240], P('seq', 'tp'), may hold values from -6 to 6
- long_seen: int32 [1], replicated, may hold values from 4096 to 8191
- short_len: int32 [3], replicated, may hold values from 1 to 504, as said below
Outputs:
- layer_out: bfloat16 [8, 4, 2560], P(None, None, 'tp')
Inputs may be any that keep to these rules, and one draw needn't show every extreme that they name: `short_len`: some short request has exactly 504 cached tokens and some exactly 1.
All inputs are finite; a program needn't handle non-finite values.
Results may differ from a plain program's by a relative error of at most 0.01.
Values may be sent and summed in bfloat16 or wider, within the bound.
No kernel may reach another device: no remote copies, remote signals or barrier semaphores. Data moves between devices by JAX's collectives and lax.ppermute only.
A program may use at most 128 MiB of HBM per device.

v0:
```python
import math

import jax
import jax.numpy as jnp
from jax import lax
from jax.sharding import PartitionSpec as P

HEADS = 32
KV_HEADS = 8
HD = 80
WIN = 4096
STEPS = 8
LONG = 1


eps_norm = 1e-05
theta_base = 10000.0
masked_score = -1e30


def rms_scaled(hidden_rows, norm_gain):
    mean_square = jnp.mean(hidden_rows * hidden_rows, axis=-1, keepdims=True)
    return hidden_rows * lax.rsqrt(mean_square + eps_norm) * norm_gain.astype(jnp.float32)


def rotate(vectors, positions):
    half_width = vectors.shape[-1] // 2
    freq_index = jnp.arange(half_width, dtype=jnp.float32)
    frequency = theta_base ** (-2.0 * freq_index / vectors.shape[-1])
    angles = positions.astype(jnp.float32)[..., None] * frequency
    view_shape = angles.shape[:2] + (1,) * (vectors.ndim - 3) + (half_width,)
    cosine_table = jnp.cos(angles).reshape(view_shape)
    sine_table = jnp.sin(angles).reshape(view_shape)
    front_part = vectors[..., :half_width]
    back_part = vectors[..., half_width:]
    return jnp.concatenate(
        [
            front_part * cosine_table - back_part * sine_table,
            back_part * cosine_table + front_part * sine_table,
        ],
        axis=-1,
    )


def partial_softmax(queries, cache_keys, cache_values, valid_mask):
    score_scale = 1.0 / math.sqrt(queries.shape[-1])
    scores = (
        jnp.einsum("trkgd,wkrd->trkgw", queries, cache_keys, preferred_element_type=jnp.float32)
        * score_scale
    )
    live_mask = valid_mask[:, :, None, None, :]
    scores = jnp.where(live_mask, scores, masked_score)
    top_score = jnp.max(scores, axis=-1)
    weights = jnp.where(live_mask, jnp.exp(scores - top_score[..., None]), 0.0)
    weight_sum = jnp.sum(weights, axis=-1)
    weighted = jnp.einsum(
        "trkgw,wkrd->trkgd",
        weights.astype(jnp.bfloat16),
        cache_values,
        preferred_element_type=jnp.float32,
    )
    return (top_score, weight_sum, weighted)


def body(
    tokens_in,
    attn_gain,
    mlp_gain,
    proj_query,
    proj_key,
    proj_value,
    proj_out,
    proj_gate,
    proj_up,
    proj_down,
    long_keys,
    long_values,
    short_keys,
    short_values,
    long_seen,
    short_len,
):
    seq_rank = lax.axis_index("seq")
    tp_rank = lax.axis_index("tp")
    local_width = tokens_in.shape[2]
    model_width = proj_query.shape[0]
    total_reqs = tokens_in.shape[1]
    group_size = HEADS // KV_HEADS
    kv_local = proj_key.shape[1] // HD
    base_pos = jnp.concatenate([long_seen, short_len])
    roll_start = long_seen % WIN
    long_slots = long_keys.shape[0]
    short_slots = short_keys.shape[0]
    long_global = seq_rank * long_slots + jnp.arange(long_slots, dtype=jnp.int32)
    long_age = (long_global[None, :] - roll_start[:, None]) % WIN
    short_global = seq_rank * short_slots + jnp.arange(short_slots, dtype=jnp.int32)
    short_live = short_global[None, :] < short_len[:, None]
    long_key_view = long_keys.reshape(long_slots, kv_local, LONG, HD)
    long_value_view = long_values.reshape(long_slots, kv_local, LONG, HD)
    short_key_view = short_keys.reshape(short_slots, kv_local, total_reqs - LONG, HD)
    short_value_view = short_values.reshape(short_slots, kv_local, total_reqs - LONG, HD)
    collected = []
    prior_keys = []
    prior_values = []
    for step_num in range(STEPS):
        token_rows = tokens_in[step_num : step_num + 1]
        block_steps = token_rows.shape[0]
        full_rows = lax.all_gather(token_rows, "tp", axis=2, tiled=True)
        normed = rms_scaled(full_rows.astype(jnp.float32), attn_gain).astype(jnp.bfloat16)
        flat_rows = normed.reshape(block_steps * total_reqs, model_width)
        steps_here = step_num + jnp.arange(block_steps, dtype=jnp.int32)
        positions = steps_here[:, None] + base_pos[None, :]
        queries = jnp.dot(flat_rows, proj_query, preferred_element_type=jnp.float32)
        queries = rotate(
            queries.reshape(block_steps, total_reqs, kv_local, group_size, HD), positions
        ).astype(jnp.bfloat16)
        key_new = jnp.dot(flat_rows, proj_key, preferred_element_type=jnp.float32)
        key_new = rotate(key_new.reshape(block_steps, total_reqs, kv_local, HD), positions).astype(
            jnp.bfloat16
        )
        value_new = jnp.dot(flat_rows, proj_value, preferred_element_type=jnp.float32)
        value_new = value_new.reshape(block_steps, total_reqs, kv_local, HD).astype(jnp.bfloat16)
        every_key = jnp.concatenate(prior_keys + [key_new], axis=0).transpose(0, 2, 1, 3)
        every_value = jnp.concatenate(prior_values + [value_new], axis=0).transpose(0, 2, 1, 3)
        token_ids = jnp.arange(every_key.shape[0], dtype=jnp.int32)
        fresh_valid = jnp.broadcast_to(
            token_ids[None, None, :] <= steps_here[:, None, None],
            (block_steps, total_reqs, every_key.shape[0]),
        )
        long_valid = long_age[None, :, :] > steps_here[:, None, None]
        short_valid = short_live[None]
        long_part = partial_softmax(queries[:, :LONG], long_key_view, long_value_view, long_valid)
        short_part = partial_softmax(
            queries[:, LONG:], short_key_view, short_value_view, short_valid
        )
        old_top = jnp.concatenate([long_part[0], short_part[0]], axis=1)
        old_sum = jnp.concatenate([long_part[1], short_part[1]], axis=1)
        old_acc = jnp.concatenate([long_part[2], short_part[2]], axis=1)
        global_top = lax.pmax(old_top, "seq")
        rescale = jnp.exp(old_top - global_top)
        old_sum, old_acc = lax.psum((old_sum * rescale, old_acc * rescale[..., None]), "seq")
        old_top = global_top
        new_top, new_sum, new_acc = partial_softmax(queries, every_key, every_value, fresh_valid)
        both_top = jnp.maximum(old_top, new_top)
        old_factor = jnp.exp(old_top - both_top)
        new_factor = jnp.exp(new_top - both_top)
        attended = (old_acc * old_factor[..., None] + new_acc * new_factor[..., None]) / (
            old_sum * old_factor + new_sum * new_factor
        )[..., None]
        attended = attended.astype(jnp.bfloat16).reshape(
            block_steps * total_reqs, kv_local * group_size * HD
        )
        head_term = jnp.dot(attended, proj_out, preferred_element_type=jnp.float32).reshape(
            block_steps, total_reqs, model_width
        )
        stream_full = full_rows.astype(jnp.float32) + lax.psum(
            head_term.astype(jnp.bfloat16), "tp"
        ).astype(jnp.float32)
        mlp_in = rms_scaled(stream_full, mlp_gain).astype(jnp.bfloat16)
        stream = lax.dynamic_slice_in_dim(
            stream_full, tp_rank * local_width, local_width, stream_full.ndim - 1
        )
        mlp_flat = mlp_in.reshape(block_steps * total_reqs, model_width)
        gate_act = jnp.dot(mlp_flat, proj_gate, preferred_element_type=jnp.float32)
        up_act = jnp.dot(mlp_flat, proj_up, preferred_element_type=jnp.float32)
        hidden_act = (jax.nn.silu(gate_act) * up_act).astype(jnp.bfloat16)
        down_term = jnp.dot(hidden_act, proj_down, preferred_element_type=jnp.float32).reshape(
            block_steps, total_reqs, model_width
        )
        result = (
            stream
            + lax.psum_scatter(
                down_term.astype(jnp.bfloat16), "tp", scatter_dimension=2, tiled=True
            ).astype(jnp.float32)
        ).astype(jnp.bfloat16)
        result, key_new, value_new = (result, key_new, value_new)
        collected.append(result)
        prior_keys = prior_keys + [key_new]
        prior_values = prior_values + [value_new]
    output = jnp.concatenate(collected, axis=0)
    return output


def solution(mesh):
    in_specs = (
        P(None, None, "tp"),
        P(),
        P(),
        P(None, "tp"),
        P(None, "tp"),
        P(None, "tp"),
        P("tp", None),
        P(None, "tp"),
        P(None, "tp"),
        P("tp", None),
        P("seq", "tp", None),
        P("seq", "tp", None),
        P("seq", "tp", None),
        P("seq", "tp", None),
        P(),
        P(),
    )
    out_specs = P(None, None, "tp")
    return jax.shard_map(body, mesh=mesh, in_specs=in_specs, out_specs=out_specs, check_vma=False)
```

profile of v0, /device:TPU:1, one launch (start us, length us, event | category | flops | bytes accessed | tf_op | source)
XLA Modules:
  0.0 886.6 jit_solution(83622997668964139)
XLA Ops:
  9.4 17.5 %all_gather.24 = bf16[1,4,2560]{1,0,2:T(2,128)(2,1)S(1)} all-gather(bf16[1,4,320]{1,0,2:T(2,128)(2,1)} %copy.291), channel_id=1, replica_groups=mesh['seq'=32,'tp'=8] {'tp'}, dimensions={2}, use_global_device_ids=true | all-gather | bytes 23040 | tf_op jit(solution)/shard_map/all_gather | solution.py:108
  29.5 14.8 %all_gather.25 = bf16[1,4,2560]{1,0,2:T(2,128)(2,1)S(1)} all-gather(bf16[1,4,320]{1,0,2:T(2,128)(2,1)} %copy.292), channel_id=1, replica_groups=mesh['seq'=32,'tp'=8] {'tp'}, dimensions={2}, use_global_device_ids=true | all-gather | bytes 23040 | tf_op jit(solution)/shard_map/all_gather | solution.py:108
  56.9 14.8 %all_gather.27 = bf16[1,4,2560]{1,0,2:T(2,128)(2,1)S(1)} all-gather(bf16[1,4,320]{1,0,2:T(2,128)(2,1)} %copy.294), channel_id=1, replica_groups=mesh['seq'=32,'tp'=8] {'tp'}, dimensions={2}, use_global_device_ids=true | all-gather | bytes 23040 | tf_op jit(solution)/shard_map/all_gather | solution.py:108
  74.8 2.7 convolution_bitcast_fusion.4
  79.0 14.9 %all_gather.26 = bf16[1,4,2560]{1,0,2:T(2,128)(2,1)S(1)} all-gather(bf16[1,4,320]{1,0,2:T(2,128)(2,1)} %copy.293), channel_id=1, replica_groups=mesh['seq'=32,'tp'=8] {'tp'}, dimensions={2}, use_global_device_ids=true | all-gather | bytes 23040 | tf_op jit(solution)/shard_map/all_gather | solution.py:108
  102.0 15.0 %all_gather.29 = bf16[1,4,2560]{1,0,2:T(2,128)(2,1)S(1)} all-gather(bf16[1,4,320]{1,0,2:T(2,128)(2,1)} %copy.296), channel_id=1, replica_groups=mesh['seq'=32,'tp'=8] {'tp'}, dimensions={2}, use_global_device_ids=true | all-gather | bytes 23040 | tf_op jit(solution)/shard_map/all_gather | solution.py:108
  118.4 2.7 convolution_bitcast_fusion.2
  122.6 15.0 %all_gather.28 = bf16[1,4,2560]{1,0,2:T(2,128)(2,1)S(1)} all-gather(bf16[1,4,320]{1,0,2:T(2,128)(2,1)} %copy.295), channel_id=1, replica_groups=mesh['seq'=32,'tp'=8] {'tp'}, dimensions={2}, use_global_device_ids=true | all-gather | bytes 23040 | tf_op jit(solution)/shard_map/all_gather | solution.py:108
  147.5 15.0 %all_gather.31 = bf16[1,4,2560]{1,0,2:T(2,128)(2,1)S(1)} all-gather(bf16[1,4,320]{1,0,2:T(2,128)(2,1)} %copy.298), channel_id=1, replica_groups=mesh['seq'=32,'tp'=8] {'tp'}, dimensions={2}, use_global_device_ids=true | all-gather | bytes 23040 | tf_op jit(solution)/shard_map/all_gather | solution.py:108
  163.9 2.7 convolution_bitcast_fusion
  168.0 15.3 %all_gather.30 = bf16[1,4,2560]{1,0,2:T(2,128)(2,1)S(1)} all-gather(bf16[1,4,320]{1,0,2:T(2,128)(2,1)} %copy.297), channel_id=1, replica_groups=mesh['seq'=32,'tp'=8] {'tp'}, dimensions={2}, use_global_device_ids=true | all-gather | bytes 23040 | tf_op jit(solution)/shard_map/all_gather | solution.py:108
  206.8 116.7 %all-reduce.1 = (f32[1,4,1,4]{3,1,2,0:T(4,128)S(1)}, f32[1,4,1,4]{3,1,2,0:T(4,128)S(1)}, f32[1,4,1,4]{3,1,2,0:T(4,128)S(1)}, f32[1,4,1,4]{3,1,2,0:T(4,128)S(1)},...) all-reduce(f32[1,4,1,4]{3,1,2,0:T(4,128)S(1)} %pad_maximum_fusion.1, ...), channel_id=1, replica_groups=mesh['seq'=32,'tp'=8] {'seq'}, use_global_device_ids=true, to_apply=%region_3.4 | all-reduce | flops 128 | bytes 1024 | tf_op jit(solution)/shard_map/pmax | solution.py:139
  324.3 110.6 %all-reduce = (f32[1,4,1,4,80]{4,3,1,0,2:T(4,128)S(1)}, f32[1,4,1,4]{3,1,2,0:T(4,128)S(1)}, f32[1,4,1,4,80]{4,3,1,0,2:T(4,128)S(1)}, f32[1,4,1,4]{3,1,2,0:T(4,12...) all-reduce(f32[1,4,1,4,80]{4,3,1,0,2:T(4,128)S(1)} %maximum_multipl, ...), channel_id=1, replica_groups=mesh['seq'=32,'tp'=8] {'seq'}, use_global_device_ids=true, to_apply=%region_4.5 | all-reduce | flops 10368 | bytes 82944 | tf_op jit(solution)/shard_map/psum | solution.py:141
  438.5 2.4 fusion
  447.9 2.4 fusion.6
  464.7 113.0 %all-reduce.5.cloned.1.call-done = (bf16[1,4,2560]{2,1,0:T(4,128)(2,1)}, bf16[1,4,2560]{2,1,0:T(4,128)(2,1)}, bf16[1,4,2560]{2,1,0:T(4,128)(2,1)}, bf16[1,4,2560...) async-done(((bf16[1,4,2560]{2,1,0:T(4,128)(2,1)}, ...) | async-done | bytes 163856 | tf_op jit(solution)/shard_map/psum | solution.py:156
  581.6 3.5 fusion.1
  592.4 3.5 fusion.3
  598.9 3.6 fusion.5
  605.6 3.6 fusion.7
  612.2 3.5 fusion.9
  618.8 3.6 fusion.11
  626.8 2.9 fusion.609
  632.9 3.5 fusion.13
  648.9 3.0 fusion.605
  655.0 3.5 fusion.15
  663.6 30.6 %reduce-scatter.29.cloned.1.call-done = bf16[320,4]{1,0:T(8,128)(2,1)} async-done(((bf16[2560,4]{1,0:T(8,128)(2,1)}), bf16[320,4]{1,0:T(8,128)(2,1)}) %reduce-scatter.29.cloned.1.call-update) | async-done | bytes 2576
  695.2 34.4 %reduce-scatter.31.cloned.1.call-done = bf16[320,4]{1,0:T(8,128)(2,1)} async-done(((bf16[2560,4]{1,0:T(8,128)(2,1)}), bf16[320,4]{1,0:T(8,128)(2,1)}) %reduce-scatter.31.cloned.1.call-update) | async-done | bytes 2576
  730.6 34.4 %reduce-scatter.33.cloned.1.call-done = bf16[320,4]{1,0:T(8,128)(2,1)} async-done(((bf16[2560,4]{1,0:T(8,128)(2,1)}), bf16[320,4]{1,0:T(8,128)(2,1)}) %reduce-scatter.33.cloned.1.call-update) | async-done | bytes 2576
  766.0 34.6 %reduce-scatter.35.cloned.1.call-done = bf16[320,4]{1,0:T(8,128)(2,1)} async-done(((bf16[2560,4]{1,0:T(8,128)(2,1)}), bf16[320,4]{1,0:T(8,128)(2,1)}) %reduce-scatter.35.cloned.1.call-update) | async-done | bytes 2576
  801.5 34.5 %reduce-scatter.37.cloned.1.call-done = bf16[320,4]{1,0:T(8,128)(2,1)} async-done(((bf16[2560,4]{1,0:T(8,128)(2,1)}), bf16[320,4]{1,0:T(8,128)(2,1)}) %reduce-scatter.37.cloned.1.call-update) | async-done | bytes 2576
  837.8 33.8 %reduce-scatter.39.cloned.1.call-done = bf16[320,4]{1,0:T(8,128)(2,1)} async-done(((bf16[2560,4]{1,0:T(8,128)(2,1)}), bf16[320,4]{1,0:T(8,128)(2,1)}) %reduce-scatter.39.cloned.1.call-update) | async-done | bytes 2576
  (522 shorter events, 159.1 us)
Async XLA Ops:
  6.5 575.1 %copy-start = (bf16[432,2560]{1,0:T(8,128)(2,1)S(1)}, bf16[432,2560]{1,0:T(8,128)(2,1)}, u32[]{:S(2)}) copy-start(bf16[432,2560]{1,0:T(8,128)(2,1)} %param.25) | copy-start | bytes 6635524
  6.5 571.2 %all-reduce.5.cloned.1.call-start = ((), (), s32[]{:S(2)}) async-start(), calls=%async_computation.16 | async-start | bytes 327680 | tf_op jit(solution)/shard_map/psum | solution.py:156
  45.0 26.7 %copy-start.2 = (bf16[1,4,2560]{2,1,0:T(4,128)(2,1)}, bf16[1,4,2560]{2,1,0:T(4,128)(2,1)S(1)}, u32[]{:S(2)}) copy-start(bf16[1,4,2560]{2,1,0:T(4,128)(2,1)S(1)} %copy.174) | copy-start | bytes 61444
  117.7 21.6 %copy-start.11 = (bf16[1,4,2560]{2,1,0:T(4,128)(2,1)}, bf16[1,4,2560]{2,1,0:T(4,128)(2,1)S(1)}, u32[]{:S(2)}) copy-start(bf16[1,4,2560]{2,1,0:T(4,128)(2,1)S(1)} %copy.223) | copy-start | bytes 61444
  168.0 21.5 %copy-start.1 = (bf16[128,1,80]{0,2,1:T(8,128)(2,1)S(1)}, bf16[128,1,80]{0,2,1:T(8,128)(2,1)}, u32[]{:S(2)}) copy-start(bf16[128,1,80]{0,2,1:T(8,128)(2,1)} %param.26) | copy-start | bytes 61444
  185.1 15.3 %copy-start.79 = (bf16[3,4,80]{2,0,1:T(4,128)(2,1)S(1)}, bf16[3,4,80]{2,0,1:T(4,128)(2,1)}, u32[]{:S(2)}) copy-start(bf16[3,4,80]{2,0,1:T(4,128)(2,1)} %fusion.258) | copy-start | bytes 5764
  185.1 15.5 %copy-start.78 = (bf16[3,4,80]{2,0,1:T(4,128)(2,1)S(1)}, bf16[3,4,80]{2,0,1:T(4,128)(2,1)}, u32[]{:S(2)}) copy-start(bf16[3,4,80]{2,0,1:T(4,128)(2,1)} %fusion.257) | copy-start | bytes 5764
  185.2 15.7 %copy-start.81 = (bf16[3,4,80]{2,0,1:T(4,128)(2,1)S(1)}, bf16[3,4,80]{2,0,1:T(4,128)(2,1)}, u32[]{:S(2)}) copy-start(bf16[3,4,80]{2,0,1:T(4,128)(2,1)} %fusion.256) | copy-start | bytes 5764
  185.2 15.9 %copy-start.80 = (bf16[3,4,80]{2,0,1:T(4,128)(2,1)S(1)}, bf16[3,4,80]{2,0,1:T(4,128)(2,1)}, u32[]{:S(2)}) copy-start(bf16[3,4,80]{2,0,1:T(4,128)(2,1)} %fusion.255) | copy-start | bytes 5764
  185.2 18.7 %copy-start.3 = (bf16[1,4,2560]{2,1,0:T(4,128)(2,1)S(1)}, bf16[1,4,2560]{2,1,0:T(4,128)(2,1)}, u32[]{:S(2)}) copy-start(bf16[1,4,2560]{2,1,0:T(4,128)(2,1)} %copy-done.2) | copy-start | bytes 61444
  185.2 18.7 %copy-start.91 = (f32[4]{0:T(128)S(1)}, f32[4]{0:T(128)}, u32[]{:S(2)}) copy-start(f32[4]{0:T(128)} %copy-done.90) | copy-start | bytes 52
  185.2 18.7 %copy-start.98 = (bf16[2560,80]{0,1:T(8,128)(2,1)S(1)}, bf16[2560,80]{0,1:T(8,128)(2,1)}, u32[]{:S(2)}) copy-start(bf16[2560,80]{0,1:T(8,128)(2,1)} %param.20) | copy-start | bytes 1228804
  185.2 19.0 %copy-start.8 = (bf16[1,4,2560]{2,1,0:T(4,128)(2,1)S(1)}, bf16[1,4,2560]{2,1,0:T(4,128)(2,1)}, u32[]{:S(2)}) copy-start(bf16[1,4,2560]{2,1,0:T(4,128)(2,1)} %copy.166) | copy-start | bytes 61444
  185.2 19.0 %copy-start.95 = (f32[4]{0:T(128)S(1)}, f32[4]{0:T(128)}, u32[]{:S(2)}) copy-start(f32[4]{0:T(128)} %copy-done.94) | copy-start | bytes 52
  186.1 18.3 %copy-start.19 = (bf16[1,4,2560]{2,1,0:T(4,128)(2,1)S(1)}, bf16[1,4,2560]{2,1,0:T(4,128)(2,1)}, u32[]{:S(2)}) copy-start(bf16[1,4,2560]{2,1,0:T(4,128)(2,1)} %copy.212) | copy-start | bytes 61444
  186.1 18.3 %copy-start.87 = (f32[4]{0:T(128)S(1)}, f32[4]{0:T(128)}, u32[]{:S(2)}) copy-start(f32[4]{0:T(128)} %copy-done.86) | copy-start | bytes 52
  186.2 18.6 %copy-start.9 = (bf16[1,4,2560]{2,1,0:T(4,128)(2,1)S(1)}, bf16[1,4,2560]{2,1,0:T(4,128)(2,1)}, u32[]{:S(2)}) copy-start(bf16[1,4,2560]{2,1,0:T(4,128)(2,1)} %copy.200) | copy-start | bytes 61444
  186.2 18.6 %copy-start.89 = (f32[4]{0:T(128)S(1)}, f32[4]{0:T(128)}, u32[]{:S(2)}) copy-start(f32[4]{0:T(128)} %copy-done.88) | copy-start | bytes 52
  188.3 16.7 %copy-start.15 = (bf16[1,4,2560]{2,1,0:T(4,128)(2,1)S(1)}, bf16[1,4,2560]{2,1,0:T(4,128)(2,1)}, u32[]{:S(2)}) copy-start(bf16[1,4,2560]{2,1,0:T(4,128)(2,1)} %copy-done.14) | copy-start | bytes 61444
  188.3 16.7 %copy-start.93 = (f32[4]{0:T(128)S(1)}, f32[4]{0:T(128)}, u32[]{:S(2)}) copy-start(f32[4]{0:T(128)} %copy-done.92) | copy-start | bytes 52
  188.3 17.0 %copy-start.6 = (bf16[1,4,2560]{2,1,0:T(4,128)(2,1)S(1)}, bf16[1,4,2560]{2,1,0:T(4,128)(2,1)}, u32[]{:S(2)}) copy-start(bf16[1,4,2560]{2,1,0:T(4,128)(2,1)} %copy-done.5) | copy-start | bytes 61444
  188.3 17.0 %copy-start.83 = (f32[4]{0:T(128)S(1)}, f32[4]{0:T(128)}, u32[]{:S(2)}) copy-start(f32[4]{0:T(128)} %copy-done.82) | copy-start | bytes 52
  204.2 232.3 %copy-start.41 = (bf16[1,4,1,4,40]{4,1,3,2,0:T(4,128)(2,1)S(1)}, bf16[1,4,1,4,40]{4,1,3,2,0:T(4,128)(2,1)}, u32[]{:S(2)}) copy-start(bf16[1,4,1,4,40]{4,1,3,2,0:T(4,128)(2,1)} %copy-done.40) | copy-start | bytes 3844
  204.2 232.3 %copy-start.43 = (bf16[1,4,1,4,40]{4,1,3,2,0:T(4,128)(2,1)S(1)}, bf16[1,4,1,4,40]{4,1,3,2,0:T(4,128)(2,1)}, u32[]{:S(2)}) copy-start(bf16[1,4,1,4,40]{4,1,3,2,0:T(4,128)(2,1)} %copy-done.42) | copy-start | bytes 3844
  464.6 197.0 %reduce-scatter.25.cloned.1.call-start = ((), (), s32[]{:S(2)}) async-start(), calls=%async_computation.8 | async-start | bytes 737280
  588.2 74.4 %reduce-scatter.27.cloned.1.call-start = ((), (), s32[]{:S(2)}) async-start(), calls=%async_computation.9 | async-start | bytes 737280
  626.8 67.5 %reduce-scatter.29.cloned.1.call-start = ((), (), s32[]{:S(2)}) async-start(), calls=%async_computation.10 | async-start | bytes 737280
  632.9 96.7 %reduce-scatter.31.cloned.1.call-start = ((), (), s32[]{:S(2)}) async-start(), calls=%async_computation.11 | async-start | bytes 737280
  639.5 125.5 %reduce-scatter.33.cloned.1.call-start = ((), (), s32[]{:S(2)}) async-start(), calls=%async_computation.12 | async-start | bytes 737280
  644.6 155.9 %reduce-scatter.35.cloned.1.call-start = ((), (), s32[]{:S(2)}) async-start(), calls=%async_computation.13 | async-start | bytes 737280
  648.9 187.2 %reduce-scatter.37.cloned.1.call-start = ((), (), s32[]{:S(2)}) async-start(), calls=%async_computation.14 | async-start | bytes 737280
  654.9 216.6 %reduce-scatter.39.cloned.1.call-start = ((), (), s32[]{:S(2)}) async-start(), calls=%async_computation.15 | async-start | bytes 737280
  (78 other events, 477.7 us)
Sparse Core Ops, SparseCore 0:
  464.8 112.9 all-reduce.4
  588.4 32.0 reduce-scatter.24
  626.9 31.9 reduce-scatter.26
  661.3 32.8 reduce-scatter.28
  696.6 32.9 reduce-scatter.30
  732.0 32.9 reduce-scatter.32
  767.5 32.9 reduce-scatter.34
  803.1 32.9 reduce-scatter.36
  838.6 32.9 reduce-scatter.38
where the time goes:
time: 892 us; the launch traced here: 887 us
  blocking collectives  350 us (39%)
  waiting for transfers between devices  315 us (35%)
  matrix products  107 us (12%)
  local copies, waits for them, and re-layouts  57.8 us (6%)
  other arithmetic  41 us (5%)
  between operations  15.4 us (2%)
    unnamed x17, waiting for transfers between devices  202 us
    all_gather x8, blocking collectives, body(): full_rows = lax.all_gather(token_rows, 'tp', axis=2, tiled=True)  122 us
    pmax x1, blocking collectives, body(): global_top = lax.pmax(old_top, 'seq')  117 us
    psum x1, waiting for transfers between devices, body(): lax.psum(head_term.astype(jnp.bfloat16), 'tp').astype(jnp.float32)  113 us
    psum x1, blocking collectives, body(): lax.psum((old_sum * rescale, old_acc * rescale[..., None]), 'seq')  111 us
    unnamed x247, local copies, waits for them, and re-layouts  45.7 us
    dot_general x8, matrix products, body(): jnp.dot(hidden_act, proj_down, preferred_element_type=jnp.float32)  28.4 us
    dot_general x8, matrix products, body(): gate_act = jnp.dot(mlp_flat, proj_gate, preferred_element_type=jnp.float32)  19.7 us
  transfers between devices with their start and end apart: 9, of which 7 were waited for; matrix products, arithmetic and copies ran while one was open for 9% of the time, Pallas kernels for 0%

commit v1 on v0

v1 whole, which is shorter than its diff:
```python
import math

import jax
import jax.numpy as jnp
import numpy as np
from jax import lax
from jax.experimental import pallas as pl
from jax.experimental.pallas import tpu as pltpu
from jax.sharding import Mesh, PartitionSpec as P

HEADS = 32
KV_HEADS = 8
GROUP = HEADS // KV_HEADS
HD = 80
HALF = HD // 2
D = 2560
WIN = 4096
STEPS = 8
REQS = 4
ROWS = STEPS * REQS
NZ, NX, NY, NC = 8, 4, 4, 2
NSEQ = NZ * NX
NTP = NY * NC
LOCAL = D // NTP
SLOTS = WIN // NSEQ
SSLOTS = 16
EPS = 1e-05
MASKED = -1e30
SEQ = ("z", "x")
TP = ("y", "c")
F32 = jnp.float32
BF16 = jnp.bfloat16
NN = (((1,), (0,)), ((), ()))
NT = (((1,), (1,)), ((), ()))
TN = (((0,), (0,)), ((), ()))


def mm(a, b, dims):
    return lax.dot_general(a, b, dims, preferred_element_type=F32)


def iota(shape, dim):
    return lax.broadcasted_iota(jnp.int32, shape, dim)


def wide_rows(piece):
    return jnp.concatenate([piece(c) for c in range(NTP)], axis=-1)


def split3(v):
    hi = v.astype(BF16).astype(F32)
    mid = (v - hi).astype(BF16).astype(F32)
    low = (v - hi - mid).astype(BF16).astype(F32)
    return hi, mid, low


def attend_kernel(
    seen_ref, len_ref, x_ref, gain_ref, freq_ref, wq_ref, wk_ref, wv_ref,
    lk_ref, lv_ref, sk_ref, sv_ref, part_ref, own_ref,
):
    z_rank = lax.axis_index("z")
    seq_rank = z_rank * NX + lax.axis_index("x")
    x_bf = wide_rows(lambda c: x_ref[c])
    x = x_bf.astype(F32)
    mean_square = jnp.mean(x * x, axis=-1, keepdims=True)
    normed = (x * lax.rsqrt(mean_square + EPS) * gain_ref[...].astype(F32)).astype(BF16)
    pick = (iota((8, ROWS), 1) == z_rank * REQS + iota((8, ROWS), 0)).astype(BF16)
    own_ref[...] = mm(pick, x_bf, NN)[:REQS]

    col = iota((HALF, ROWS), 1)
    req = col & 3
    base = jnp.where(req == 0, seen_ref[0], jnp.where(req == 1, len_ref[0], jnp.where(req == 2, len_ref[1], len_ref[2])))
    angles = ((col >> 2) + base).astype(F32) * freq_ref[...]
    cos = jnp.cos(angles)
    sin = jnp.sin(angles)

    def rope(v):
        front, back = v[:HALF], v[HALF:]
        return jnp.concatenate([front * cos - back * sin, back * cos + front * sin], axis=0)

    q_t = mm(wq_ref[...], normed, NT)
    k_t = rope(mm(wk_ref[...], normed, NT)).astype(BF16)
    v_t = mm(wv_ref[...], normed, NT).astype(BF16)
    q_all = jnp.concatenate([rope(q_t[h * HD : (h + 1) * HD]) for h in range(GROUP)], axis=1)
    q = q_all.T.astype(BF16)

    scale = 1.0 / math.sqrt(HD)
    n_rows = GROUP * ROWS
    sk = jnp.concatenate([sk_ref[:, r * HD : (r + 1) * HD] for r in range(REQS - 1)], axis=0)
    sv = jnp.concatenate([sv_ref[:, r * HD : (r + 1) * HD] for r in range(REQS - 1)], axis=0)
    s_long = mm(q, lk_ref[...], NN) * scale
    s_short = mm(q, sk, NT) * scale
    s_new = mm(q, k_t, NN) * scale

    def row_ids(shape):
        row = iota(shape, 0)
        return row & 3, (row >> 2) & 7

    r, t = row_ids(s_long.shape)
    age = (seq_rank * SLOTS + iota(s_long.shape, 1) - seen_ref[0]) & (WIN - 1)
    see_long = (r == 0) & (age > t)
    r, t = row_ids(s_short.shape)
    j = iota(s_short.shape, 1)
    n_cached = jnp.where(r == 1, len_ref[0], jnp.where(r == 2, len_ref[1], len_ref[2]))
    see_short = ((j >> 4) + 1 == r) & (seq_rank * SSLOTS + (j & 15) < n_cached)
    r, t = row_ids(s_new.shape)
    j = iota(s_new.shape, 1)
    see_new = ((j & 3) == r) & ((j >> 2) <= t) & (seq_rank == 0)
    s_long = jnp.where(see_long, s_long, MASKED)
    s_short = jnp.where(see_short, s_short, MASKED)
    s_new = jnp.where(see_new, s_new, MASKED)
    top = jnp.maximum(
        jnp.maximum(jnp.max(s_long, axis=-1, keepdims=True), jnp.max(s_short, axis=-1, keepdims=True)),
        jnp.max(s_new, axis=-1, keepdims=True),
    )
    w_long = jnp.where(see_long, jnp.exp(s_long - top), 0.0)
    w_short = jnp.where(see_short, jnp.exp(s_short - top), 0.0)
    w_new = jnp.where(see_new, jnp.exp(s_new - top), 0.0)
    total = (
        jnp.sum(w_long, axis=-1, keepdims=True)
        + jnp.sum(w_short, axis=-1, keepdims=True)
        + jnp.sum(w_new, axis=-1, keepdims=True)
    )
    acc = (
        mm(w_long.astype(BF16), lv_ref[...], NT)
        + mm(w_short.astype(BF16), sv, NN)
        + mm(w_new.astype(BF16), v_t, NT)
    )
    top_a, top_b, top_c = split3(top)
    sum_a, sum_b, _ = split3(total)
    acc = jnp.concatenate([acc, jnp.zeros((n_rows, 128 - HD), F32)], axis=1)
    lane = iota(acc.shape, 1)
    for k, v in enumerate((top_a, top_b, top_c, sum_a, sum_b)):
        acc = jnp.where(lane == HD + k, v, acc)
    for step in range(STEPS):
        rows = jnp.concatenate(
            [acc[h * ROWS + step * REQS : h * ROWS + (step + 1) * REQS] for h in range(GROUP)], axis=0
        ).astype(BF16)
        for x_to in range(NX):
            part_ref[step * NX + x_to] = rows


def combine_kernel(part_ref, wo_ref, out_ref):
    part = part_ref[...]
    src = iota((128, 256), 0)
    dst = iota((128, 256), 1)
    spread = (
        ((dst < 128) & (src >= HD) & (src < HD + 3)) | ((dst >= 128) & (src >= HD + 3) & (src < HD + 5))
    ).astype(BF16)
    stats = mm(part.reshape(NSEQ * 16, 128), spread, NN)
    top = stats[:, :128].reshape(NSEQ, 16, 128)
    total = stats[:, 128:].reshape(NSEQ, 16, 128)
    factor = jnp.exp(top - jnp.max(top, axis=0, keepdims=True))
    weighted = jnp.sum(part.astype(F32) * factor, axis=0)
    attended = weighted / jnp.sum(total * factor, axis=0)
    attended = jnp.concatenate([attended[h * REQS : (h + 1) * REQS, :HD] for h in range(GROUP)], axis=1)
    term = mm(attended.astype(BF16), wo_ref[...], NN).astype(BF16)
    for to in range(NTP):
        out_ref[to] = term


def mlp_kernel(part_ref, own_ref, gain_ref, wg_ref, wu_ref, wd_ref, out_ref):
    tp_rank = lax.axis_index("y") * NC + lax.axis_index("c")
    head_sum = jnp.sum(part_ref[...].astype(F32), axis=0)
    stream = own_ref[...] + head_sum
    mean_square = jnp.mean(stream * stream, axis=-1, keepdims=True)
    mlp_in = stream * lax.rsqrt(mean_square + EPS) * gain_ref[...].astype(F32)
    mlp_in = jnp.concatenate([mlp_in, jnp.zeros((16 - REQS, D), F32)], axis=0).astype(BF16)
    gate = mm(wg_ref[...], mlp_in, NT)
    up = mm(wu_ref[...], mlp_in, NT)
    hidden = (gate / (1.0 + jnp.exp(-gate)) * up).astype(BF16)
    down = mm(hidden, wd_ref[...], TN)[:REQS]
    for to in range(NTP):
        cols = slice(to * LOCAL, (to + 1) * LOCAL)
        piece = (down[:, cols] + jnp.where(tp_rank == to, head_sum[:, cols], 0.0)).astype(BF16)
        for z_to in range(NZ):
            out_ref[z_to * NTP + to] = piece


def call(kernel, out_shape, n_smem, args):
    specs = [pl.BlockSpec(memory_space=pltpu.SMEM)] * n_smem + [pl.BlockSpec(memory_space=pltpu.VMEM)] * (
        len(args) - n_smem
    )
    return pl.pallas_call(
        kernel,
        out_shape=out_shape,
        in_specs=specs,
        compiler_params=pltpu.CompilerParams(vmem_limit_bytes=24 * 1024 * 1024),
    )(*args)


def body(
    tokens_in, attn_gain, mlp_gain, proj_query, proj_key, proj_value, proj_out, proj_gate, proj_up,
    proj_down, long_keys, long_values, short_keys, short_values, long_seen, short_len,
):
    freq = 10000.0 ** (-2.0 * np.arange(HALF) / HD)
    freq = jnp.asarray(np.repeat(freq[:, None], ROWS, axis=1).astype(np.float32))
    flat = tokens_in.reshape(ROWS, LOCAL)
    x_all = lax.all_to_all(jnp.broadcast_to(flat[None], (NTP, ROWS, LOCAL)), TP, 0, 0, tiled=True)
    parts, own = call(
        attend_kernel,
        (jax.ShapeDtypeStruct((NSEQ, 16, 128), BF16), jax.ShapeDtypeStruct((REQS, D), F32)),
        2,
        (
            long_seen, short_len, x_all, attn_gain.reshape(1, D), freq,
            proj_query.T, proj_key.T, proj_value.T,
            long_keys.reshape(SLOTS, HD).T, long_values.reshape(SLOTS, HD).T,
            short_keys.reshape(SSLOTS, 3 * HD), short_values.reshape(SSLOTS, 3 * HD),
        ),
    )
    parts = lax.all_to_all(parts, SEQ, 0, 0, tiled=True)
    terms = call(combine_kernel, jax.ShapeDtypeStruct((NTP, REQS, D), BF16), 0, (parts, proj_out))
    terms = lax.all_to_all(terms, TP, 0, 0, tiled=True)
    pieces = call(
        mlp_kernel,
        jax.ShapeDtypeStruct((NZ * NTP, REQS, LOCAL), BF16),
        0,
        (terms, own, mlp_gain.reshape(1, D), proj_gate.T, proj_up.T, proj_down),
    )
    pieces = lax.all_to_all(pieces, ("z",) + TP, 0, 0, tiled=True)
    total = jnp.sum(pieces.reshape(NZ, NTP, REQS, LOCAL).astype(F32), axis=1)
    return (tokens_in.astype(F32) + total).astype(BF16)


def solution(mesh):
    fine = Mesh(mesh.devices.reshape(NZ, NX, NY, NC), ("z", "x", "y", "c"))
    cols = P(None, TP)
    rows = P(TP, None)
    cache = P(SEQ, TP, None)
    in_specs = (
        P(None, None, TP), P(), P(), cols, cols, cols, rows, cols, cols, rows,
        cache, cache, cache, cache, P(), P(),
    )
    return jax.shard_map(body, mesh=fine, in_specs=in_specs, out_specs=P(None, None, TP), check_vma=False)
```

time: 892 us -> 80.7 us (0.09)
  blocking collectives: 350 us -> 36.1 us
  waiting for transfers between devices: 315 us -> 10.1 us
  matrix products: 107 us -> 0 us
  local copies, waits for them, and re-layouts: 57.8 us -> 14.5 us
  other arithmetic: 41 us -> 0.72 us
  between operations: 15.4 us -> 0.69 us
  starting transfers between devices: 0.56 us -> 12.1 us
    unnamed x17 -> x0, waiting for transfers between devices: 202 us -> none
    all_gather x8 -> x0, blocking collectives: 122 us -> none  [body(): full_rows = lax.all_gather(token_rows, 'tp', axis=2, tiled=True)]
    pmax x1 -> x0, blocking collectives: 117 us -> none  [body(): global_top = lax.pmax(old_top, 'seq')]
    psum x1 -> x0, waiting for transfers between devices: 113 us -> none  [body(): lax.psum(head_term.astype(jnp.bfloat16), 'tp').astype(jnp.float32)]
    psum x1 -> x0, blocking collectives: 111 us -> none  [body(): lax.psum((old_sum * rescale, old_acc * rescale[..., None]), 'seq')]
    dot_general x95 -> x0, matrix products: 107 us -> none  [the longest x8 28.4 us: body(): jnp.dot(hidden_act, proj_down, preferred_element_type=jnp.float32)]
    all_to_all x0 -> x2, blocking collectives: none -> 36.1 us  [the longest x1 19.7 us: body(): parts = lax.all_to_all(parts, SEQ, 0, 0, tiled=True)]
    unnamed x247 -> x30, local copies, waits for them, and re-layouts: 45.7 us -> 12.3 us
  transfers between devices with their start and end apart: 9 -> 2, of which waited for: 7 -> 2; matrix products, arithmetic and copies ran while one was open for 9% -> 1% of each run, Pallas kernels for 0% -> 0%
where the time goes in v1:
time: 80.7 us; the launch traced here: 79.8 us
  blocking collectives  36.1 us (45%)
  local copies, waits for them, and re-layouts  14.5 us (18%)
  starting transfers between devices  12.1 us (15%)
  waiting for transfers between devices  10.1 us (13%)
  Pallas kernels  5.57 us (7%)
    all_to_all x1, blocking collectives, body(): parts = lax.all_to_all(parts, SEQ, 0, 0, tiled=True)  19.7 us
    all_to_all x1, blocking collectives, body(): pieces = lax.all_to_all(pieces, ('z',) + TP, 0, 0, tiled=True)  16.4 us
    unnamed x30, local copies, waits for them, and re-layouts  12.3 us
    all_to_all x1, starting transfers between devices, body(): lax.all_to_all(jnp.broadcast_to(flat[None], (NTP, ROWS, LOCAL)), TP, 0, 0...  6.49 us
    all_to_all x1, starting transfers between devices, body(): terms = lax.all_to_all(terms, TP, 0, 0, tiled=True)  5.65 us
    pallas_call x3, Pallas kernels, call(): pl.pallas_call(kernel, out_shape=out_shape, in_specs=specs, compiler_para...  5.57 us
    all_to_all x1, waiting for transfers between devices, body(): terms = lax.all_to_all(terms, TP, 0, 0, tiled=True)  5.56 us
    all_to_all x1, waiting for transfers between devices, body(): lax.all_to_all(jnp.broadcast_to(flat[None], (NTP, ROWS, LOCAL)), TP, 0, 0...  4.53 us
  transfers between devices with their start and end apart: 2, of which 2 were waited for; matrix products, arithmetic and copies ran while one was open for 1% of the time, Pallas kernels for 0%

profile of v1, /device:TPU:1, one launch (start us, length us, event | category | flops | bytes accessed | tf_op | source)
XLA Modules:
  0.0 79.8 jit_solution(5294131048681289023)
XLA Ops:
  0.0 0.8 broadcast_in_dim.7
  0.8 0.7 broadcast_in_dim.8
  1.4 6.5 %all-to-all-start = ((bf16[8,32,320]{2,1,0:T(8,128)(2,1)}), bf16[8,32,320]{2,1,0:T(8,128)(2,1)S(1)}, u32[]{:S(2)}, u32[]{:S(2)}) async-start(bf16[8,32,320]{2,1,0:T(8,128)(2,1)} %broadcast_in_dim.8), calls=%async_computation | async-start | bytes 393216 | tf_op jit(solution)/shard_map/all_to_all | solution.py:199
  7.9 0.7 reshape.22.gain_ref
  9.3 4.5 %all-to-all-done.x_ref = bf16[8,32,320]{2,1,0:T(8,128)(2,1)S(1)} async-done(((bf16[8,32,320]{2,1,0:T(8,128)(2,1)}), bf16[8,32,320]{2,1,0:T(8,128)(2,1)S(1)}, u32[]{:S(2)}, u32[]{:S(2)}) %all-to-all-start) | async-done | bytes 163872 | tf_op jit(solution)/shard_map/all_to_all | solution.py:199
  13.8 1.4 %copy-done.3 = bf16[2560,320]{0,1:T(8,128)(2,1)S(1)} copy-done((bf16[2560,320]{0,1:T(8,128)(2,1)S(1)}, bf16[2560,320]{0,1:T(8,128)(2,1)}, u32[]{:S(2)}) %copy-start.3) | copy-done | bytes 1638424
  15.3 0.0 copy-start.5
  15.3 1.0 %copy-done.5 = bf16[2560,80]{0,1:T(8,128)(2,1)S(1)} copy-done((bf16[2560,80]{0,1:T(8,128)(2,1)S(1)}, bf16[2560,80]{0,1:T(8,128)(2,1)}, u32[]{:S(2)}) %copy-start.5) | copy-done | bytes 409624
  16.3 0.0 copy-start.6
  16.3 1.0 %copy-done.6 = bf16[2560,80]{0,1:T(8,128)(2,1)S(1)} copy-done((bf16[2560,80]{0,1:T(8,128)(2,1)S(1)}, bf16[2560,80]{0,1:T(8,128)(2,1)}, u32[]{:S(2)}) %copy-start.6) | copy-done | bytes 409624
  17.3 0.0 copy-start.7
  17.3 0.7 copy-done.7
  18.0 0.7 copy-done.8
  18.7 0.7 copy-done.9
  19.4 0.7 copy-done.10
  20.1 0.7 copy-done.11
  20.8 0.7 copy-done.12
  21.5 2.2 %shard_map.163 = (bf16[32,16,128]{2,1,0:T(8,128)(2,1)S(1)}, f32[4,2560]{1,0:T(4,128)S(1)}) custom-call(s32[1]{0:T(128)S(6)} %copy.18.seen_ref, s32[3]{0:T(128)S(1)} %copy-done.12, bf16[8,32,320]{2,1,0:T(8,128)(2,1)S(1)} %all-to-all-done.x_ref, bf16[1,2560]{1,0:T(2,128)(2,1)S(1)} %reshape.22.gain_ref, f32[40,32]{1,0:T(8,128)S(1)} %copy-done.9, ...), custom_call_target="tpu_custom_call" | custom-call | tf_op jit(solution)/shard_map/pallas_call | solution.py:184
  23.7 19.7 %all_to_all.20.part_ref = bf16[32,16,128]{2,1,0:T(8,128)(2,1)S(1)} all-to-all(bf16[32,16,128]{2,1,0:T(8,128)(2,1)S(1)} %get-tuple-element.7), channel_id=1, replica_groups=mesh['z'=8,'x'=4,'y'=4,'c'=2] {'z','x'}, dimensions={0} | all-to-all | bytes 262144 | tf_op jit(solution)/shard_map/all_to_all | solution.py:211
  43.4 1.4 %copy-done.4 = bf16[320,2560]{1,0:T(8,128)(2,1)S(1)} copy-done((bf16[320,2560]{1,0:T(8,128)(2,1)S(1)}, bf16[320,2560]{1,0:T(8,128)(2,1)}, u32[]{:S(2)}) %copy-start.4) | copy-done | bytes 1638424
  44.8 1.5 %shard_map.164 = bf16[8,4,2560]{2,1,0:T(4,128)(2,1)} custom-call(bf16[32,16,128]{2,1,0:T(8,128)(2,1)S(1)} %all_to_all.20.part_ref, bf16[320,2560]{1,0:T(8,128)(2,1)S(1)} %copy-done.4), custom_call_target="tpu_custom_call" | custom-call | tf_op jit(solution)/shard_map/pallas_call | solution.py:184
  46.2 5.6 %all-to-all-start.2 = ((bf16[8,4,2560]{2,1,0:T(4,128)(2,1)}), bf16[8,4,2560]{2,1,0:T(4,128)(2,1)S(1)}, u32[]{:S(2)}, u32[]{:S(2)}) async-start(bf16[8,4,2560]{2,1,0:T(4,128)(2,1)} %shard_map.164), calls=%async_computation.2 | async-start | bytes 327680 | tf_op jit(solution)/shard_map/all_to_all | solution.py:213
  51.9 0.0 copy-done.14
  51.9 5.6 %all-to-all-done.2.part_ref = bf16[8,4,2560]{2,1,0:T(4,128)(2,1)S(1)} async-done(((bf16[8,4,2560]{2,1,0:T(4,128)(2,1)}), bf16[8,4,2560]{2,1,0:T(4,128)(2,1)S(1)}, u32[]{:S(2)}, u32[]{:S(2)}) %all-to-all-start.2) | async-done | bytes 163872 | tf_op jit(solution)/shard_map/all_to_all | solution.py:213
  57.5 0.0 copy-done
  57.5 1.6 %copy-done.1 = bf16[2560,432]{0,1:T(8,128)(2,1)S(1)} copy-done((bf16[2560,432]{0,1:T(8,128)(2,1)S(1)}, bf16[2560,432]{0,1:T(8,128)(2,1)}, u32[]{:S(2)}) %copy-start.1) | copy-done | bytes 2211864
  59.1 1.6 %copy-done.2 = bf16[432,2560]{1,0:T(8,128)(2,1)S(1)} copy-done((bf16[432,2560]{1,0:T(8,128)(2,1)S(1)}, bf16[432,2560]{1,0:T(8,128)(2,1)}, u32[]{:S(2)}) %copy-start.2) | copy-done | bytes 2211864
  60.7 1.9 %shard_map.165 = bf16[64,4,320]{2,1,0:T(4,128)(2,1)S(1)} custom-call(bf16[8,4,2560]{2,1,0:T(4,128)(2,1)S(1)} %all-to-all-done.2.part_ref, f32[4,2560]{1,0:T(4,128)S(1)} %get-tuple-element.8.own_ref, bf16[1,2560]{1,0:T(2,128)(2,1)S(1)} %reshape.27.gain_ref, bf16[432,2560]{1,0:T(8,128)(2,1)S(1)} %bitcast.16, bf16[432,2560]{1,0:T(8,128)(2,1)S(1)} %bitcast.17, ...), custom_call_target="tpu_custom_call" | custom-call | tf_op jit(solution)/shard_map/pallas_call | solution.py:184
  62.7 16.4 %all_to_all.21 = bf16[64,4,320]{2,1,0:T(4,128)(2,1)S(1)} all-to-all(bf16[64,4,320]{2,1,0:T(4,128)(2,1)S(1)} %shard_map.165), channel_id=1, replica_groups=mesh['z'=8,'x'=4,'y'=4,'c'=2] {'z','y','c'}, dimensions={0} | all-to-all | bytes 327680 | tf_op jit(solution)/shard_map/all_to_all | solution.py:220
  79.1 0.1 convert_reduce_fusion
  79.2 0.0 copy-done.13
  79.2 0.6 add_convert_fusion
  (13 shorter events, 0.0 us)
Async XLA Ops:
  1.4 12.4 %all-to-all-start = ((bf16[8,32,320]{2,1,0:T(8,128)(2,1)}), bf16[8,32,320]{2,1,0:T(8,128)(2,1)S(1)}, u32[]{:S(2)}, u32[]{:S(2)}) async-start(bf16[8,32,320]{2,1,0:T(8,128)(2,1)} %broadcast_in_dim.8), calls=%async_computation | async-start | bytes 393216 | tf_op jit(solution)/shard_map/all_to_all | solution.py:199
  13.8 1.4 %copy-start.3 = (bf16[2560,320]{0,1:T(8,128)(2,1)S(1)}, bf16[2560,320]{0,1:T(8,128)(2,1)}, u32[]{:S(2)}) copy-start(bf16[2560,320]{0,1:T(8,128)(2,1)} %param.20) | copy-start | bytes 4915204
  15.3 1.0 %copy-start.5 = (bf16[2560,80]{0,1:T(8,128)(2,1)S(1)}, bf16[2560,80]{0,1:T(8,128)(2,1)}, u32[]{:S(2)}) copy-start(bf16[2560,80]{0,1:T(8,128)(2,1)} %param.21) | copy-start | bytes 1228804
  16.3 1.0 %copy-start.6 = (bf16[2560,80]{0,1:T(8,128)(2,1)S(1)}, bf16[2560,80]{0,1:T(8,128)(2,1)}, u32[]{:S(2)}) copy-start(bf16[2560,80]{0,1:T(8,128)(2,1)} %param.22) | copy-start | bytes 1228804
  17.3 0.7 copy-start.7
  18.0 0.7 copy-start.8
  18.7 0.7 copy-start.9
  19.4 0.7 copy-start.10
  20.1 0.7 copy-start.11
  20.8 0.7 copy-start.12
  21.5 30.4 %copy-start.14 = (bf16[2560]{0:T(1024)(128)(2,1)S(1)}, bf16[2560]{0:T(1024)(128)(2,1)}, u32[]{:S(2)}) copy-start(bf16[2560]{0:T(1024)(128)(2,1)} %param.19) | copy-start | bytes 15364
  21.5 36.0 %copy-start = (bf16[2560,432]{0,1:T(8,128)(2,1)S(1)}, bf16[2560,432]{0,1:T(8,128)(2,1)}, u32[]{:S(2)}) copy-start(bf16[2560,432]{0,1:T(8,128)(2,1)} %param.24) | copy-start | bytes 6635524
  43.4 1.4 %copy-start.4 = (bf16[320,2560]{1,0:T(8,128)(2,1)S(1)}, bf16[320,2560]{1,0:T(8,128)(2,1)}, u32[]{:S(2)}) copy-start(bf16[320,2560]{1,0:T(8,128)(2,1)} %wo_ref.1) | copy-start | bytes 4915204
  46.2 11.2 %all-to-all-start.2 = ((bf16[8,4,2560]{2,1,0:T(4,128)(2,1)}), bf16[8,4,2560]{2,1,0:T(4,128)(2,1)S(1)}, u32[]{:S(2)}, u32[]{:S(2)}) async-start(bf16[8,4,2560]{2,1,0:T(4,128)(2,1)} %shard_map.164), calls=%async_computation.2 | async-start | bytes 327680 | tf_op jit(solution)/shard_map/all_to_all | solution.py:213
  57.5 1.6 %copy-start.1 = (bf16[2560,432]{0,1:T(8,128)(2,1)S(1)}, bf16[2560,432]{0,1:T(8,128)(2,1)}, u32[]{:S(2)}) copy-start(bf16[2560,432]{0,1:T(8,128)(2,1)} %param.25) | copy-start | bytes 6635524
  59.1 1.6 %copy-start.2 = (bf16[432,2560]{1,0:T(8,128)(2,1)S(1)}, bf16[432,2560]{1,0:T(8,128)(2,1)}, u32[]{:S(2)}) copy-start(bf16[432,2560]{1,0:T(8,128)(2,1)} %wd_ref.1) | copy-start | bytes 6635524
  60.7 18.4 %copy-start.13 = (bf16[8,4,320]{2,1,0:T(4,128)(2,1)S(1)}, bf16[8,4,320]{2,1,0:T(4,128)(2,1)}, u32[]{:S(2)}) copy-start(bf16[8,4,320]{2,1,0:T(4,128)(2,1)} %param.17) | copy-start | bytes 61444

commit v2 on v1

--- a/solution.py
+++ b/solution.py
@@ -54,19 +54,36 @@
     return hi, mid, low
 
 
+def spread_kernel(tokens_ref, out_ref):
+    rows = jnp.concatenate([tokens_ref[t].astype(F32) for t in range(STEPS)], axis=0).astype(BF16)
+    for to in range(NTP):
+        out_ref[to] = rows
+
+
+def finish_kernel(piece_ref, tokens_ref, out_ref):
+    for z_from in range(NZ):
+        total = jnp.sum(piece_ref[z_from * NTP : (z_from + 1) * NTP].astype(F32), axis=0)
+        out_ref[z_from] = (tokens_ref[z_from].astype(F32) + total).astype(BF16)
+
+
 def attend_kernel(
-    seen_ref, len_ref, x_ref, gain_ref, freq_ref, wq_ref, wk_ref, wv_ref,
-    lk_ref, lv_ref, sk_ref, sv_ref, part_ref, own_ref,
+    seen_hbm, len_hbm, x_ref, gain_ref, freq_ref, wq_ref, wk_ref, wv_ref,
+    lk_ref, lv_ref, sk_ref, sv_ref, part_ref, own_ref, seen_ref, len_ref, sems,
 ):
+    loads = [pltpu.make_async_copy(seen_hbm, seen_ref, sems.at[0]), pltpu.make_async_copy(len_hbm, len_ref, sems.at[1])]
+    for load in loads:
+        load.start()
     z_rank = lax.axis_index("z")
     seq_rank = z_rank * NX + lax.axis_index("x")
     x_bf = wide_rows(lambda c: x_ref[c])
     x = x_bf.astype(F32)
     mean_square = jnp.mean(x * x, axis=-1, keepdims=True)
-    normed = (x * lax.rsqrt(mean_square + EPS) * gain_ref[...].astype(F32)).astype(BF16)
+    normed = (x * lax.rsqrt(mean_square + EPS) * gain_ref[...].astype(F32).reshape(1, D)).astype(BF16)
     pick = (iota((8, ROWS), 1) == z_rank * REQS + iota((8, ROWS), 0)).astype(BF16)
     own_ref[...] = mm(pick, x_bf, NN)[:REQS]
 
+    for load in loads:
+        load.wait()
     col = iota((HALF, ROWS), 1)
     req = col & 3
     base = jnp.where(req == 0, seen_ref[0], jnp.where(req == 1, len_ref[0], jnp.where(req == 2, len_ref[1], len_ref[2])))
@@ -164,7 +181,7 @@
     head_sum = jnp.sum(part_ref[...].astype(F32), axis=0)
     stream = own_ref[...] + head_sum
     mean_square = jnp.mean(stream * stream, axis=-1, keepdims=True)
-    mlp_in = stream * lax.rsqrt(mean_square + EPS) * gain_ref[...].astype(F32)
+    mlp_in = stream * lax.rsqrt(mean_square + EPS) * gain_ref[...].astype(F32).reshape(1, D)
     mlp_in = jnp.concatenate([mlp_in, jnp.zeros((16 - REQS, D), F32)], axis=0).astype(BF16)
     gate = mm(wg_ref[...], mlp_in, NT)
     up = mm(wu_ref[...], mlp_in, NT)
@@ -177,15 +194,17 @@
             out_ref[z_to * NTP + to] = piece
 
 
-def call(kernel, out_shape, n_smem, args):
-    specs = [pl.BlockSpec(memory_space=pltpu.SMEM)] * n_smem + [pl.BlockSpec(memory_space=pltpu.VMEM)] * (
+def call(kernel, out_shape, n_smem, args, scratch=()):
+    specs = [pl.BlockSpec(memory_space=pltpu.HBM)] * n_smem + [pl.BlockSpec(memory_space=pltpu.VMEM)] * (
         len(args) - n_smem
     )
     return pl.pallas_call(
         kernel,
         out_shape=out_shape,
         in_specs=specs,
-        compiler_params=pltpu.CompilerParams(vmem_limit_bytes=24 * 1024 * 1024),
+        scratch_shapes=scratch,
+        cost_estimate=pl.CostEstimate(flops=50_000_000_000, bytes_accessed=100_000_000, transcendentals=0),
+        compiler_params=pltpu.CompilerParams(vmem_limit_bytes=16 * 1024 * 1024),
     )(*args)
 
 
@@ -195,18 +214,19 @@
 ):
     freq = 10000.0 ** (-2.0 * np.arange(HALF) / HD)
     freq = jnp.asarray(np.repeat(freq[:, None], ROWS, axis=1).astype(np.float32))
-    flat = tokens_in.reshape(ROWS, LOCAL)
-    x_all = lax.all_to_all(jnp.broadcast_to(flat[None], (NTP, ROWS, LOCAL)), TP, 0, 0, tiled=True)
+    copies = call(spread_kernel, jax.ShapeDtypeStruct((NTP, ROWS, LOCAL), BF16), 0, (tokens_in,))
+    x_all = lax.all_to_all(copies, TP, 0, 0, tiled=True)
     parts, own = call(
         attend_kernel,
         (jax.ShapeDtypeStruct((NSEQ, 16, 128), BF16), jax.ShapeDtypeStruct((REQS, D), F32)),
         2,
         (
-            long_seen, short_len, x_all, attn_gain.reshape(1, D), freq,
+            long_seen, short_len, x_all, attn_gain, freq,
             proj_query.T, proj_key.T, proj_value.T,
             long_keys.reshape(SLOTS, HD).T, long_values.reshape(SLOTS, HD).T,
             short_keys.reshape(SSLOTS, 3 * HD), short_values.reshape(SSLOTS, 3 * HD),
         ),
+        (pltpu.SMEM((1,), jnp.int32), pltpu.SMEM((3,), jnp.int32), pltpu.SemaphoreType.DMA((2,))),
     )
     parts = lax.all_to_all(parts, SEQ, 0, 0, tiled=True)
     terms = call(combine_kernel, jax.ShapeDtypeStruct((NTP, REQS, D), BF16), 0, (parts, proj_out))
@@ -215,11 +235,10 @@
         mlp_kernel,
         jax.ShapeDtypeStruct((NZ * NTP, REQS, LOCAL), BF16),
         0,
-        (terms, own, mlp_gain.reshape(1, D), proj_gate.T, proj_up.T, proj_down),
+        (terms, own, mlp_gain, proj_gate.T, proj_up.T, proj_down),
     )
     pieces = lax.all_to_all(pieces, ("z",) + TP, 0, 0, tiled=True)
-    total = jnp.sum(pieces.reshape(NZ, NTP, REQS, LOCAL).astype(F32), axis=1)
-    return (tokens_in.astype(F32) + total).astype(BF16)
+    return call(finish_kernel, jax.ShapeDtypeStruct((STEPS, REQS, LOCAL), BF16), 0, (pieces, tokens_in))
 
 
 def solution(mesh):

time: 80.7 us -> 66.7 us (0.83)
  local copies, waits for them, and re-layouts: 14.5 us -> 0.95 us
  blocking collectives: 36.1 us -> 46.7 us
  starting transfers between devices: 12.1 us -> 6.49 us
  waiting for transfers between devices: 10.1 us -> 5.23 us
    unnamed x30 -> x34, local copies, waits for them, and re-layouts: 12.3 us -> 0.95 us
    all_to_all x0 -> x1, blocking collectives: none -> 10.6 us  [body(): terms = lax.all_to_all(terms, TP, 0, 0, tiled=True)]
    all_to_all x2 -> x1, starting transfers between devices: 12.1 us -> 6.49 us  [body(): x_all = lax.all_to_all(copies, TP, 0, 0, tiled=True)]
    all_to_all x2 -> x1, waiting for transfers between devices: 10.1 us -> 5.23 us  [body(): x_all = lax.all_to_all(copies, TP, 0, 0, tiled=True)]
    broadcast_in_dim x2 -> x0, local copies, waits for them, and re-layouts: 1.45 us -> none  [body(): jnp.broadcast_to(flat[None], (NTP, ROWS, LOCAL))]
    pallas_call x3 -> x5, Pallas kernels: 5.57 us -> 6.22 us  [call(): pl.pallas_call(kernel, out_shape=out_shape, in_specs=specs, scratch_shape...]
  transfers between devices with their start and end apart: 2 -> 1, of which waited for: 2 -> 1; matrix products, arithmetic and copies ran while one was open for 1% -> 0% of each run, Pallas kernels for 0% -> 0%
where the time goes in v2:
time: 66.7 us; the launch traced here: 66.4 us
  blocking collectives  46.7 us (70%)
  starting transfers between devices  6.49 us (10%)
  Pallas kernels  6.22 us (9%)
  waiting for transfers between devices  5.23 us (8%)
  local copies, waits for them, and re-layouts  0.95 us (1%)
  between operations  0.81 us (1%)
    all_to_all x1, blocking collectives, body(): parts = lax.all_to_all(parts, SEQ, 0, 0, tiled=True)  19.7 us
    all_to_all x1, blocking collectives, body(): pieces = lax.all_to_all(pieces, ('z',) + TP, 0, 0, tiled=True)  16.4 us
    all_to_all x1, blocking collectives, body(): terms = lax.all_to_all(terms, TP, 0, 0, tiled=True)  10.6 us
    all_to_all x1, starting transfers between devices, body(): x_all = lax.all_to_all(copies, TP, 0, 0, tiled=True)  6.49 us
    pallas_call x5, Pallas kernels, call(): pl.pallas_call(kernel, out_shape=out_shape, in_specs=specs, scratch_shape...  6.22 us
    all_to_all x1, waiting for transfers between devices, body(): x_all = lax.all_to_all(copies, TP, 0, 0, tiled=True)  5.23 us
  transfers between devices with their start and end apart: 1, of which 1 were waited for; matrix products, arithmetic and copies ran while one was open for 0% of the time, Pallas kernels for 0%

profile of v2, /device:TPU:1, one launch (start us, length us, event | category | flops | bytes accessed | tf_op | source)
XLA Modules:
  0.0 66.4 jit_solution(12574800372603748296)
XLA Ops:
  0.0 0.0 copy-start.7
  0.0 0.9 %copy-done.7 = bf16[8,4,320]{2,1,0:T(4,128)(2,1)S(1)} copy-done((bf16[8,4,320]{2,1,0:T(4,128)(2,1)S(1)}, bf16[8,4,320]{2,1,0:T(4,128)(2,1)}, u32[]{:S(2)}) %copy-start.7) | copy-done | bytes 20504
  0.9 0.0 copy-start.13
  0.9 0.0 copy-start.15
  0.9 0.0 copy-start.16
  0.9 0.7 %shard_map.163 = bf16[8,32,320]{2,1,0:T(8,128)(2,1)} custom-call(bf16[8,4,320]{2,1,0:T(4,128)(2,1)S(1)} %copy-done.7), custom_call_target="tpu_custom_call" | custom-call | flops 49999998976 | bytes 100000000 | tf_op jit(solution)/shard_map/pallas_call | solution.py:201
  1.6 6.5 %all-to-all-start = ((bf16[8,32,320]{2,1,0:T(8,128)(2,1)}), bf16[8,32,320]{2,1,0:T(8,128)(2,1)S(1)}, u32[]{:S(2)}, u32[]{:S(2)}) async-start(bf16[8,32,320]{2,1,0:T(8,128)(2,1)} %shard_map.163), calls=%async_computation | async-start | bytes 393216 | tf_op jit(solution)/shard_map/all_to_all | solution.py:218
  8.8 5.2 %all-to-all-done.x_ref = bf16[8,32,320]{2,1,0:T(8,128)(2,1)S(1)} async-done(((bf16[8,32,320]{2,1,0:T(8,128)(2,1)}), bf16[8,32,320]{2,1,0:T(8,128)(2,1)S(1)}, u32[]{:S(2)}, u32[]{:S(2)}) %all-to-all-start) | async-done | bytes 163872 | tf_op jit(solution)/shard_map/all_to_all | solution.py:218
  14.0 0.0 copy-done.3
  14.0 0.0 copy-done.5
  14.0 0.0 copy-done.6
  14.0 0.0 copy-done.9
  14.0 0.0 copy-done.10
  14.0 0.0 copy-done.11
  14.0 0.0 copy-done.12
  14.1 0.0 copy-done.13
  14.1 0.0 copy-done.15
  14.1 0.0 copy-done.16
  14.1 0.0 copy-start.4
  14.1 2.1 %shard_map.164 = (bf16[32,16,128]{2,1,0:T(8,128)(2,1)S(1)}, f32[4,2560]{1,0:T(4,128)S(1)}) custom-call(s32[1]{0:T(128)S(6)} %copy.18.seen_hbm, s32[3]{0:T(128)S(1)} %copy-done.15, bf16[8,32,320]{2,1,0:T(8,128)(2,1)S(1)} %all-to-all-done.x_ref, bf16[2560]{0:T(1024)(128)(2,1)S(1)} %copy-done.13, f32[40,32]{1,0:T(8,128)S(1)} %copy-done.16, ...), custom_call_target="tpu_custom_call" | custom-call | flops 49999998976 | bytes 100000000 | tf_op jit(solution)/shard_map/pallas_call | solution.py:201
  16.2 19.7 %all_to_all.20.part_ref = bf16[32,16,128]{2,1,0:T(8,128)(2,1)S(1)} all-to-all(bf16[32,16,128]{2,1,0:T(8,128)(2,1)S(1)} %get-tuple-element.7), channel_id=1, replica_groups=mesh['z'=8,'x'=4,'y'=4,'c'=2] {'z','x'}, dimensions={0} | all-to-all | bytes 262144 | tf_op jit(solution)/shard_map/all_to_all | solution.py:231
  35.9 0.0 copy-done.4
  35.9 0.0 copy-start.14
  35.9 0.8 %shard_map.165 = bf16[8,4,2560]{2,1,0:T(4,128)(2,1)S(1)} custom-call(bf16[32,16,128]{2,1,0:T(8,128)(2,1)S(1)} %all_to_all.20.part_ref, bf16[320,2560]{1,0:T(8,128)(2,1)S(1)} %copy-done.4), custom_call_target="tpu_custom_call" | custom-call | flops 49999998976 | bytes 100000000 | tf_op jit(solution)/shard_map/pallas_call | solution.py:201
  36.7 10.6 %all_to_all.21.part_ref = bf16[8,4,2560]{2,1,0:T(4,128)(2,1)S(1)} all-to-all(bf16[8,4,2560]{2,1,0:T(4,128)(2,1)S(1)} %shard_map.165), channel_id=1, replica_groups=mesh['z'=8,'x'=4,'y'=4,'c'=2] {'y','c'}, dimensions={0} | all-to-all | bytes 327680 | tf_op jit(solution)/shard_map/all_to_all | solution.py:233
  47.3 0.0 copy-done
  47.3 0.0 copy-done.1
  47.3 0.0 copy-done.2
  47.3 0.0 copy-start.8
  47.3 1.9 %shard_map.166 = bf16[64,4,320]{2,1,0:T(4,128)(2,1)S(1)} custom-call(bf16[8,4,2560]{2,1,0:T(4,128)(2,1)S(1)} %all_to_all.21.part_ref, f32[4,2560]{1,0:T(4,128)S(1)} %get-tuple-element.8.own_ref, bf16[2560]{0:T(1024)(128)(2,1)S(1)} %copy-done.14, bf16[432,2560]{1,0:T(8,128)(2,1)S(1)} %bitcast.13, bf16[432,2560]{1,0:T(8,128)(2,1)S(1)} %bitcast.14, ...), custom_call_target="tpu_custom_call" | custom-call | flops 49999998976 | bytes 100000000 | tf_op jit(solution)/shard_map/pallas_call | solution.py:201
  49.3 16.4 %all_to_all.22.piece_ref = bf16[64,4,320]{2,1,0:T(4,128)(2,1)S(1)} all-to-all(bf16[64,4,320]{2,1,0:T(4,128)(2,1)S(1)} %shard_map.166), channel_id=1, replica_groups=mesh['z'=8,'x'=4,'y'=4,'c'=2] {'z','y','c'}, dimensions={0} | all-to-all | bytes 327680 | tf_op jit(solution)/shard_map/all_to_all | solution.py:240
  65.7 0.7 %shard_map.167 = bf16[8,4,320]{2,1,0:T(4,128)(2,1)} custom-call(bf16[64,4,320]{2,1,0:T(4,128)(2,1)S(1)} %all_to_all.22.piece_ref, bf16[8,4,320]{2,1,0:T(4,128)(2,1)S(1)} %copy-done.8), custom_call_target="tpu_custom_call" | custom-call | flops 49999998976 | bytes 100000000 | tf_op jit(solution)/shard_map/pallas_call | solution.py:201
  (12 shorter events, 0.0 us)
Async XLA Ops:
  0.0 14.0 %copy-start.3 = (bf16[2560,320]{0,1:T(8,128)(2,1)S(1)}, bf16[2560,320]{0,1:T(8,128)(2,1)}, u32[]{:S(2)}) copy-start(bf16[2560,320]{0,1:T(8,128)(2,1)} %param.20) | copy-start | bytes 4915204
  0.0 14.0 %copy-start.5 = (bf16[2560,80]{0,1:T(8,128)(2,1)S(1)}, bf16[2560,80]{0,1:T(8,128)(2,1)}, u32[]{:S(2)}) copy-start(bf16[2560,80]{0,1:T(8,128)(2,1)} %param.21) | copy-start | bytes 1228804
  0.0 14.0 %copy-start.6 = (bf16[2560,80]{0,1:T(8,128)(2,1)S(1)}, bf16[2560,80]{0,1:T(8,128)(2,1)}, u32[]{:S(2)}) copy-start(bf16[2560,80]{0,1:T(8,128)(2,1)} %param.22) | copy-start | bytes 1228804
  0.0 0.9 %copy-start.7 = (bf16[8,4,320]{2,1,0:T(4,128)(2,1)S(1)}, bf16[8,4,320]{2,1,0:T(4,128)(2,1)}, u32[]{:S(2)}) copy-start(bf16[8,4,320]{2,1,0:T(4,128)(2,1)} %tokens_ref.3) | copy-start | bytes 61444
  0.9 13.1 %copy-start.9 = (bf16[128,1,80]{0,2,1:T(8,128)(2,1)S(1)}, bf16[128,1,80]{0,2,1:T(8,128)(2,1)}, u32[]{:S(2)}) copy-start(bf16[128,1,80]{0,2,1:T(8,128)(2,1)} %param.27) | copy-start | bytes 61444
  0.9 13.1 %copy-start.10 = (bf16[128,1,80]{0,2,1:T(8,128)(2,1)S(1)}, bf16[128,1,80]{0,2,1:T(8,128)(2,1)}, u32[]{:S(2)}) copy-start(bf16[128,1,80]{0,2,1:T(8,128)(2,1)} %param.28) | copy-start | bytes 61444
  0.9 13.1 %copy-start.11 = (bf16[16,1,240]{2,0,1:T(8,128)(2,1)S(1)}, bf16[16,1,240]{2,0,1:T(8,128)(2,1)}, u32[]{:S(2)}) copy-start(bf16[16,1,240]{2,0,1:T(8,128)(2,1)} %param.29) | copy-start | bytes 23044
  0.9 13.1 %copy-start.12 = (bf16[16,1,240]{2,0,1:T(8,128)(2,1)S(1)}, bf16[16,1,240]{2,0,1:T(8,128)(2,1)}, u32[]{:S(2)}) copy-start(bf16[16,1,240]{2,0,1:T(8,128)(2,1)} %param.30) | copy-start | bytes 23044
  0.9 13.1 %copy-start.13 = (bf16[2560]{0:T(1024)(128)(2,1)S(1)}, bf16[2560]{0:T(1024)(128)(2,1)}, u32[]{:S(2)}) copy-start(bf16[2560]{0:T(1024)(128)(2,1)} %gain_ref.2) | copy-start | bytes 15364
  0.9 13.1 %copy-start.15 = (s32[3]{0:T(128)S(1)}, s32[3]{0:T(128)}, u32[]{:S(2)}) copy-start(s32[3]{0:T(128)} %len_hbm.1) | copy-start | bytes 40
  0.9 13.1 %copy-start.16 = (f32[40,32]{1,0:T(8,128)S(1)}, f32[40,32]{1,0:T(8,128)}, u32[]{:S(2)}) copy-start(f32[40,32]{1,0:T(8,128)} %constant.2.clone.freq_ref) | copy-start | bytes 15364
  1.6 12.4 %all-to-all-start = ((bf16[8,32,320]{2,1,0:T(8,128)(2,1)}), bf16[8,32,320]{2,1,0:T(8,128)(2,1)S(1)}, u32[]{:S(2)}, u32[]{:S(2)}) async-start(bf16[8,32,320]{2,1,0:T(8,128)(2,1)} %shard_map.163), calls=%async_computation | async-start | bytes 393216 | tf_op jit(solution)/shard_map/all_to_all | solution.py:218
  14.1 21.8 %copy-start.4 = (bf16[320,2560]{1,0:T(8,128)(2,1)S(1)}, bf16[320,2560]{1,0:T(8,128)(2,1)}, u32[]{:S(2)}) copy-start(bf16[320,2560]{1,0:T(8,128)(2,1)} %wo_ref.1) | copy-start | bytes 4915204
  35.9 11.4 %copy-start = (bf16[2560,432]{0,1:T(8,128)(2,1)S(1)}, bf16[2560,432]{0,1:T(8,128)(2,1)}, u32[]{:S(2)}) copy-start(bf16[2560,432]{0,1:T(8,128)(2,1)} %param.24) | copy-start | bytes 6635524
  35.9 11.4 %copy-start.1 = (bf16[2560,432]{0,1:T(8,128)(2,1)S(1)}, bf16[2560,432]{0,1:T(8,128)(2,1)}, u32[]{:S(2)}) copy-start(bf16[2560,432]{0,1:T(8,128)(2,1)} %param.25) | copy-start | bytes 6635524
  35.9 11.4 %copy-start.2 = (bf16[432,2560]{1,0:T(8,128)(2,1)S(1)}, bf16[432,2560]{1,0:T(8,128)(2,1)}, u32[]{:S(2)}) copy-start(bf16[432,2560]{1,0:T(8,128)(2,1)} %wd_ref.1) | copy-start | bytes 6635524
  35.9 11.4 %copy-start.14 = (bf16[2560]{0:T(1024)(128)(2,1)S(1)}, bf16[2560]{0:T(1024)(128)(2,1)}, u32[]{:S(2)}) copy-start(bf16[2560]{0:T(1024)(128)(2,1)} %gain_ref.3) | copy-start | bytes 15364
  47.3 18.4 %copy-start.8 = (bf16[8,4,320]{2,1,0:T(4,128)(2,1)S(1)}, bf16[8,4,320]{2,1,0:T(4,128)(2,1)}, u32[]{:S(2)}) copy-start(bf16[8,4,320]{2,1,0:T(4,128)(2,1)} %tokens_ref.3) | copy-start | bytes 61444

commit v3 on v2

--- a/solution.py
+++ b/solution.py
@@ -18,7 +18,9 @@
 STEPS = 8
 REQS = 4
 ROWS = STEPS * REQS
-NZ, NX, NY, NC = 8, 4, 4, 2
+NH, NL, NX, NY, NC = 4, 2, 4, 4, 2
+NZ = NH * NL
+NG = NL * NX
 NSEQ = NZ * NX
 NTP = NY * NC
 LOCAL = D // NTP
@@ -26,7 +28,8 @@
 SSLOTS = 16
 EPS = 1e-05
 MASKED = -1e30
-SEQ = ("z", "x")
+SEQ = ("zh", "zl", "x")
+TEAM = ("zl", "x")
 TP = ("y", "c")
 F32 = jnp.float32
 BF16 = jnp.bfloat16
@@ -61,9 +64,9 @@
 
 
 def finish_kernel(piece_ref, tokens_ref, out_ref):
-    for z_from in range(NZ):
-        total = jnp.sum(piece_ref[z_from * NTP : (z_from + 1) * NTP].astype(F32), axis=0)
-        out_ref[z_from] = (tokens_ref[z_from].astype(F32) + total).astype(BF16)
+    for step in range(STEPS):
+        total = jnp.sum(piece_ref[step * NTP : (step + 1) * NTP].astype(F32), axis=0)
+        out_ref[step] = (tokens_ref[step].astype(F32) + total).astype(BF16)
 
 
 def attend_kernel(
@@ -73,13 +76,13 @@
     loads = [pltpu.make_async_copy(seen_hbm, seen_ref, sems.at[0]), pltpu.make_async_copy(len_hbm, len_ref, sems.at[1])]
     for load in loads:
         load.start()
-    z_rank = lax.axis_index("z")
-    seq_rank = z_rank * NX + lax.axis_index("x")
+    team_rank = lax.axis_index("zl") * NX + lax.axis_index("x")
+    seq_rank = lax.axis_index("zh") * NG + team_rank
     x_bf = wide_rows(lambda c: x_ref[c])
     x = x_bf.astype(F32)
     mean_square = jnp.mean(x * x, axis=-1, keepdims=True)
     normed = (x * lax.rsqrt(mean_square + EPS) * gain_ref[...].astype(F32).reshape(1, D)).astype(BF16)
-    pick = (iota((8, ROWS), 1) == z_rank * REQS + iota((8, ROWS), 0)).astype(BF16)
+    pick = (iota((8, ROWS), 1) == team_rank * REQS + iota((8, ROWS), 0)).astype(BF16)
     own_ref[...] = mm(pick, x_bf, NN)[:REQS]
 
     for load in loads:
@@ -153,8 +156,8 @@
         rows = jnp.concatenate(
             [acc[h * ROWS + step * REQS : h * ROWS + (step + 1) * REQS] for h in range(GROUP)], axis=0
         ).astype(BF16)
-        for x_to in range(NX):
-            part_ref[step * NX + x_to] = rows
+        for zh_to in range(NH):
+            part_ref[zh_to * NG + step] = rows
 
 
 def combine_kernel(part_ref, wo_ref, out_ref):
@@ -190,8 +193,8 @@
     for to in range(NTP):
         cols = slice(to * LOCAL, (to + 1) * LOCAL)
         piece = (down[:, cols] + jnp.where(tp_rank == to, head_sum[:, cols], 0.0)).astype(BF16)
-        for z_to in range(NZ):
-            out_ref[z_to * NTP + to] = piece
+        for g_to in range(NG):
+            out_ref[g_to * NTP + to] = piece
 
 
 def call(kernel, out_shape, n_smem, args, scratch=()):
@@ -233,16 +236,16 @@
     terms = lax.all_to_all(terms, TP, 0, 0, tiled=True)
     pieces = call(
         mlp_kernel,
-        jax.ShapeDtypeStruct((NZ * NTP, REQS, LOCAL), BF16),
+        jax.ShapeDtypeStruct((NG * NTP, REQS, LOCAL), BF16),
         0,
         (terms, own, mlp_gain, proj_gate.T, proj_up.T, proj_down),
     )
-    pieces = lax.all_to_all(pieces, ("z",) + TP, 0, 0, tiled=True)
+    pieces = lax.all_to_all(pieces, TEAM + TP, 0, 0, tiled=True)
     return call(finish_kernel, jax.ShapeDtypeStruct((STEPS, REQS, LOCAL), BF16), 0, (pieces, tokens_in))
 
 
 def solution(mesh):
-    fine = Mesh(mesh.devices.reshape(NZ, NX, NY, NC), ("z", "x", "y", "c"))
+    fine = Mesh(mesh.devices.reshape(NH, NL, NX, NY, NC), SEQ + TP)
     cols = P(None, TP)
     rows = P(TP, None)
     cache = P(SEQ, TP, None)

time: 66.7 us -> 64 us (0.960)
  blocking collectives: 46.7 us -> 44 us
    all_to_all x1, blocking collectives: 16.4 us -> 13.8 us  [body(): pieces = lax.all_to_all(pieces, TEAM + TP, 0, 0, tiled=True)]
where the time goes in v3:
time: 64 us; the launch traced here: 63.7 us
  blocking collectives  44 us (69%)
  starting transfers between devices  6.49 us (10%)
  Pallas kernels  6.22 us (10%)
  waiting for transfers between devices  5.23 us (8%)
  local copies, waits for them, and re-layouts  0.95 us (1%)
  between operations  0.81 us (1%)
    all_to_all x1, blocking collectives, body(): parts = lax.all_to_all(parts, SEQ, 0, 0, tiled=True)  19.7 us
    all_to_all x1, blocking collectives, body(): pieces = lax.all_to_all(pieces, TEAM + TP, 0, 0, tiled=True)  13.8 us
    all_to_all x1, blocking collectives, body(): terms = lax.all_to_all(terms, TP, 0, 0, tiled=True)  10.6 us
    all_to_all x1, starting transfers between devices, body(): x_all = lax.all_to_all(copies, TP, 0, 0, tiled=True)  6.49 us
    pallas_call x5, Pallas kernels, call(): pl.pallas_call(kernel, out_shape=out_shape, in_specs=specs, scratch_shape...  6.22 us
    all_to_all x1, waiting for transfers between devices, body(): x_all = lax.all_to_all(copies, TP, 0, 0, tiled=True)  5.23 us
  transfers between devices with their start and end apart: 1, of which 1 were waited for; matrix products, arithmetic and copies ran while one was open for 0% of the time, Pallas kernels for 0%

profile of v3, /device:TPU:1, one launch (start us, length us, event | category | flops | bytes accessed | tf_op | source)
XLA Modules:
  0.0 63.7 jit_solution(5652600420654152510)
XLA Ops:
  0.0 0.0 copy-start.7
  0.0 0.9 %copy-done.7 = bf16[8,4,320]{2,1,0:T(4,128)(2,1)S(1)} copy-done((bf16[8,4,320]{2,1,0:T(4,128)(2,1)S(1)}, bf16[8,4,320]{2,1,0:T(4,128)(2,1)}, u32[]{:S(2)}) %copy-start.7) | copy-done | bytes 20504
  0.9 0.0 copy-start.13
  0.9 0.0 copy-start.15
  0.9 0.0 copy-start.16
  0.9 0.7 %shard_map.163 = bf16[8,32,320]{2,1,0:T(8,128)(2,1)} custom-call(bf16[8,4,320]{2,1,0:T(4,128)(2,1)S(1)} %copy-done.7), custom_call_target="tpu_custom_call" | custom-call | flops 49999998976 | bytes 100000000 | tf_op jit(solution)/shard_map/pallas_call | solution.py:204
  1.6 6.5 %all-to-all-start = ((bf16[8,32,320]{2,1,0:T(8,128)(2,1)}), bf16[8,32,320]{2,1,0:T(8,128)(2,1)S(1)}, u32[]{:S(2)}, u32[]{:S(2)}) async-start(bf16[8,32,320]{2,1,0:T(8,128)(2,1)} %shard_map.163), calls=%async_computation | async-start | bytes 393216 | tf_op jit(solution)/shard_map/all_to_all | solution.py:221
  8.8 5.2 %all-to-all-done.x_ref = bf16[8,32,320]{2,1,0:T(8,128)(2,1)S(1)} async-done(((bf16[8,32,320]{2,1,0:T(8,128)(2,1)}), bf16[8,32,320]{2,1,0:T(8,128)(2,1)S(1)}, u32[]{:S(2)}, u32[]{:S(2)}) %all-to-all-start) | async-done | bytes 163872 | tf_op jit(solution)/shard_map/all_to_all | solution.py:221
  14.0 0.0 copy-done.3
  14.0 0.0 copy-done.5
  14.0 0.0 copy-done.6
  14.0 0.0 copy-done.9
  14.0 0.0 copy-done.10
  14.0 0.0 copy-done.11
  14.0 0.0 copy-done.12
  14.1 0.0 copy-done.13
  14.1 0.0 copy-done.15
  14.1 0.0 copy-done.16
  14.1 0.0 copy-start.4
  14.1 2.1 %shard_map.164 = (bf16[32,16,128]{2,1,0:T(8,128)(2,1)S(1)}, f32[4,2560]{1,0:T(4,128)S(1)}) custom-call(s32[1]{0:T(128)S(6)} %copy.18.seen_hbm, s32[3]{0:T(128)S(1)} %copy-done.15, bf16[8,32,320]{2,1,0:T(8,128)(2,1)S(1)} %all-to-all-done.x_ref, bf16[2560]{0:T(1024)(128)(2,1)S(1)} %copy-done.13, f32[40,32]{1,0:T(8,128)S(1)} %copy-done.16, ...), custom_call_target="tpu_custom_call" | custom-call | flops 49999998976 | bytes 100000000 | tf_op jit(solution)/shard_map/pallas_call | solution.py:204
  16.2 19.7 %all_to_all.20.part_ref = bf16[32,16,128]{2,1,0:T(8,128)(2,1)S(1)} all-to-all(bf16[32,16,128]{2,1,0:T(8,128)(2,1)S(1)} %get-tuple-element.7), channel_id=1, replica_groups=mesh['zh'=4,'zl'=2,'x'=4,'y'=4,'c'=2] {'zh','zl','x'}, dimensions={0} | all-to-all | bytes 262144 | tf_op jit(solution)/shard_map/all_to_all | solution.py:234
  35.9 0.0 copy-done.4
  35.9 0.0 copy-start.14
  35.9 0.8 %shard_map.165 = bf16[8,4,2560]{2,1,0:T(4,128)(2,1)S(1)} custom-call(bf16[32,16,128]{2,1,0:T(8,128)(2,1)S(1)} %all_to_all.20.part_ref, bf16[320,2560]{1,0:T(8,128)(2,1)S(1)} %copy-done.4), custom_call_target="tpu_custom_call" | custom-call | flops 49999998976 | bytes 100000000 | tf_op jit(solution)/shard_map/pallas_call | solution.py:204
  36.7 10.6 %all_to_all.21.part_ref = bf16[8,4,2560]{2,1,0:T(4,128)(2,1)S(1)} all-to-all(bf16[8,4,2560]{2,1,0:T(4,128)(2,1)S(1)} %shard_map.165), channel_id=1, replica_groups=mesh['zh'=4,'zl'=2,'x'=4,'y'=4,'c'=2] {'y','c'}, dimensions={0} | all-to-all | bytes 327680 | tf_op jit(solution)/shard_map/all_to_all | solution.py:236
  47.3 0.0 copy-done
  47.3 0.0 copy-done.1
  47.3 0.0 copy-done.2
  47.3 0.0 copy-start.8
  47.3 1.9 %shard_map.166 = bf16[64,4,320]{2,1,0:T(4,128)(2,1)S(1)} custom-call(bf16[8,4,2560]{2,1,0:T(4,128)(2,1)S(1)} %all_to_all.21.part_ref, f32[4,2560]{1,0:T(4,128)S(1)} %get-tuple-element.8.own_ref, bf16[2560]{0:T(1024)(128)(2,1)S(1)} %copy-done.14, bf16[432,2560]{1,0:T(8,128)(2,1)S(1)} %bitcast.13, bf16[432,2560]{1,0:T(8,128)(2,1)S(1)} %bitcast.14, ...), custom_call_target="tpu_custom_call" | custom-call | flops 49999998976 | bytes 100000000 | tf_op jit(solution)/shard_map/pallas_call | solution.py:204
  49.3 13.8 %all_to_all.22.piece_ref = bf16[64,4,320]{2,1,0:T(4,128)(2,1)S(1)} all-to-all(bf16[64,4,320]{2,1,0:T(4,128)(2,1)S(1)} %shard_map.166), channel_id=1, replica_groups=mesh['zh'=4,'zl'=2,'x'=4,'y'=4,'c'=2] {'zl','x','y','c'}, dimensions={0} | all-to-all | bytes 327680 | tf_op jit(solution)/shard_map/all_to_all | solution.py:243
  63.0 0.7 %shard_map.167 = bf16[8,4,320]{2,1,0:T(4,128)(2,1)} custom-call(bf16[64,4,320]{2,1,0:T(4,128)(2,1)S(1)} %all_to_all.22.piece_ref, bf16[8,4,320]{2,1,0:T(4,128)(2,1)S(1)} %copy-done.8), custom_call_target="tpu_custom_call" | custom-call | flops 49999998976 | bytes 100000000 | tf_op jit(solution)/shard_map/pallas_call | solution.py:204
  (12 shorter events, 0.0 us)
Async XLA Ops:
  0.0 14.0 %copy-start.3 = (bf16[2560,320]{0,1:T(8,128)(2,1)S(1)}, bf16[2560,320]{0,1:T(8,128)(2,1)}, u32[]{:S(2)}) copy-start(bf16[2560,320]{0,1:T(8,128)(2,1)} %param.20) | copy-start | bytes 4915204
  0.0 14.0 %copy-start.5 = (bf16[2560,80]{0,1:T(8,128)(2,1)S(1)}, bf16[2560,80]{0,1:T(8,128)(2,1)}, u32[]{:S(2)}) copy-start(bf16[2560,80]{0,1:T(8,128)(2,1)} %param.21) | copy-start | bytes 1228804
  0.0 14.0 %copy-start.6 = (bf16[2560,80]{0,1:T(8,128)(2,1)S(1)}, bf16[2560,80]{0,1:T(8,128)(2,1)}, u32[]{:S(2)}) copy-start(bf16[2560,80]{0,1:T(8,128)(2,1)} %param.22) | copy-start | bytes 1228804
  0.0 0.9 %copy-start.7 = (bf16[8,4,320]{2,1,0:T(4,128)(2,1)S(1)}, bf16[8,4,320]{2,1,0:T(4,128)(2,1)}, u32[]{:S(2)}) copy-start(bf16[8,4,320]{2,1,0:T(4,128)(2,1)} %tokens_ref.3) | copy-start | bytes 61444
  0.9 13.1 %copy-start.9 = (bf16[128,1,80]{0,2,1:T(8,128)(2,1)S(1)}, bf16[128,1,80]{0,2,1:T(8,128)(2,1)}, u32[]{:S(2)}) copy-start(bf16[128,1,80]{0,2,1:T(8,128)(2,1)} %param.27) | copy-start | bytes 61444
  0.9 13.1 %copy-start.10 = (bf16[128,1,80]{0,2,1:T(8,128)(2,1)S(1)}, bf16[128,1,80]{0,2,1:T(8,128)(2,1)}, u32[]{:S(2)}) copy-start(bf16[128,1,80]{0,2,1:T(8,128)(2,1)} %param.28) | copy-start | bytes 61444
  0.9 13.1 %copy-start.11 = (bf16[16,1,240]{2,0,1:T(8,128)(2,1)S(1)}, bf16[16,1,240]{2,0,1:T(8,128)(2,1)}, u32[]{:S(2)}) copy-start(bf16[16,1,240]{2,0,1:T(8,128)(2,1)} %param.29) | copy-start | bytes 23044
  0.9 13.1 %copy-start.12 = (bf16[16,1,240]{2,0,1:T(8,128)(2,1)S(1)}, bf16[16,1,240]{2,0,1:T(8,128)(2,1)}, u32[]{:S(2)}) copy-start(bf16[16,1,240]{2,0,1:T(8,128)(2,1)} %param.30) | copy-start | bytes 23044
  0.9 13.1 %copy-start.13 = (bf16[2560]{0:T(1024)(128)(2,1)S(1)}, bf16[2560]{0:T(1024)(128)(2,1)}, u32[]{:S(2)}) copy-start(bf16[2560]{0:T(1024)(128)(2,1)} %gain_ref.2) | copy-start | bytes 15364
  0.9 13.1 %copy-start.15 = (s32[3]{0:T(128)S(1)}, s32[3]{0:T(128)}, u32[]{:S(2)}) copy-start(s32[3]{0:T(128)} %len_hbm.1) | copy-start | bytes 40
  0.9 13.1 %copy-start.16 = (f32[40,32]{1,0:T(8,128)S(1)}, f32[40,32]{1,0:T(8,128)}, u32[]{:S(2)}) copy-start(f32[40,32]{1,0:T(8,128)} %constant.2.clone.freq_ref) | copy-start | bytes 15364
  1.6 12.4 %all-to-all-start = ((bf16[8,32,320]{2,1,0:T(8,128)(2,1)}), bf16[8,32,320]{2,1,0:T(8,128)(2,1)S(1)}, u32[]{:S(2)}, u32[]{:S(2)}) async-start(bf16[8,32,320]{2,1,0:T(8,128)(2,1)} %shard_map.163), calls=%async_computation | async-start | bytes 393216 | tf_op jit(solution)/shard_map/all_to_all | solution.py:221
  14.1 21.8 %copy-start.4 = (bf16[320,2560]{1,0:T(8,128)(2,1)S(1)}, bf16[320,2560]{1,0:T(8,128)(2,1)}, u32[]{:S(2)}) copy-start(bf16[320,2560]{1,0:T(8,128)(2,1)} %wo_ref.1) | copy-start | bytes 4915204
  35.9 11.4 %copy-start = (bf16[2560,432]{0,1:T(8,128)(2,1)S(1)}, bf16[2560,432]{0,1:T(8,128)(2,1)}, u32[]{:S(2)}) copy-start(bf16[2560,432]{0,1:T(8,128)(2,1)} %param.24) | copy-start | bytes 6635524
  35.9 11.4 %copy-start.1 = (bf16[2560,432]{0,1:T(8,128)(2,1)S(1)}, bf16[2560,432]{0,1:T(8,128)(2,1)}, u32[]{:S(2)}) copy-start(bf16[2560,432]{0,1:T(8,128)(2,1)} %param.25) | copy-start | bytes 6635524
  35.9 11.4 %copy-start.2 = (bf16[432,2560]{1,0:T(8,128)(2,1)S(1)}, bf16[432,2560]{1,0:T(8,128)(2,1)}, u32[]{:S(2)}) copy-start(bf16[432,2560]{1,0:T(8,128)(2,1)} %wd_ref.1) | copy-start | bytes 6635524
  35.9 11.4 %copy-start.14 = (bf16[2560]{0:T(1024)(128)(2,1)S(1)}, bf16[2560]{0:T(1024)(128)(2,1)}, u32[]{:S(2)}) copy-start(bf16[2560]{0:T(1024)(128)(2,1)} %gain_ref.3) | copy-start | bytes 15364
  47.3 15.7 %copy-start.8 = (bf16[8,4,320]{2,1,0:T(4,128)(2,1)S(1)}, bf16[8,4,320]{2,1,0:T(4,128)(2,1)}, u32[]{:S(2)}) copy-start(bf16[8,4,320]{2,1,0:T(4,128)(2,1)} %tokens_ref.3) | copy-start | bytes 61444

commit v4 on v3

v4 whole, which is shorter than its diff:
```python
import math

import jax
import jax.numpy as jnp
import numpy as np
from jax import lax
from jax.experimental import pallas as pl
from jax.experimental.pallas import tpu as pltpu
from jax.sharding import Mesh, PartitionSpec as P

HEADS = 32
KV_HEADS = 8
GROUP = HEADS // KV_HEADS
HD = 80
HALF = HD // 2
D = 2560
WIN = 4096
STEPS = 8
REQS = 4
ROWS = STEPS * REQS
NY, NC = 4, 2
SEQ_SIZES = {"zh": 4, "zl": 2, "xh": 2, "xl": 2}
SEQ = tuple(SEQ_SIZES)
TEAM = ('zl', 'xh', 'xl')
NG = math.prod(SEQ_SIZES[a] for a in TEAM)
TOK = STEPS * REQS // NG
NSEQ = math.prod(SEQ_SIZES.values())
NTP = NY * NC
LOCAL = D // NTP
SLOTS = WIN // NSEQ
SSLOTS = 16
EPS = 1e-05
MASKED = -1e30
TP = ("y", "c")
F32 = jnp.float32
BF16 = jnp.bfloat16
NN = (((1,), (0,)), ((), ()))
NT = (((1,), (1,)), ((), ()))
TN = (((0,), (0,)), ((), ()))


def mm(a, b, dims):
    return lax.dot_general(a, b, dims, preferred_element_type=F32)


def iota(shape, dim):
    return lax.broadcasted_iota(jnp.int32, shape, dim)


def wide_rows(piece):
    return jnp.concatenate([piece(c) for c in range(NTP)], axis=-1)


def rank_in(axes):
    rank = 0
    for a in axes:
        rank = rank * SEQ_SIZES[a] + lax.axis_index(a)
    return rank


def team_of(seq_rank):
    at = dict(zip(SEQ, np.unravel_index(seq_rank, tuple(SEQ_SIZES.values()))))
    rank = 0
    for a in TEAM:
        rank = rank * SEQ_SIZES[a] + int(at[a])
    return rank


def split3(v):
    hi = v.astype(BF16).astype(F32)
    mid = (v - hi).astype(BF16).astype(F32)
    low = (v - hi - mid).astype(BF16).astype(F32)
    return hi, mid, low


def spread_kernel(tokens_ref, out_ref, after_ref):
    after_ref[...] = jnp.zeros(after_ref.shape, F32)
    rows = jnp.concatenate([tokens_ref[t].astype(F32) for t in range(STEPS)], axis=0)
    packed = jnp.concatenate(
        [rows[:, :128], rows[:, 128:256], jnp.concatenate([rows[: ROWS // 2, 256:], rows[ROWS // 2 :, 256:]], axis=1)], axis=0
    ).astype(BF16)
    for to in range(NTP):
        out_ref[to] = packed


def unpack_rows(packed):
    last = packed[2 * ROWS :]
    tail = jnp.concatenate([last[:, :64], last[:, 64:]], axis=0)
    return jnp.concatenate([packed[:ROWS], packed[ROWS : 2 * ROWS], tail], axis=1)


def finish_kernel(piece_ref, tokens_ref, out_ref):
    for team in range(NG):
        total = jnp.sum(piece_ref[team * NTP : (team + 1) * NTP].astype(F32), axis=0)
        rows = [
            jnp.concatenate([total[2 * p], total[2 * p + 1], total[4][:, 64 * p : 64 * p + 64]], axis=1) for p in range(2)
        ]
        out_ref[team] = (tokens_ref[team].astype(F32) + jnp.concatenate(rows, axis=0)).astype(BF16)


def table_kernel(
    after_ref, seen_hbm, len_hbm, freq_ref, cos_ref, sin_ref, hide_long_ref, hide_short_ref, hide_new_ref, seen_ref, len_ref, sems,
):
    loads = [pltpu.make_async_copy(seen_hbm, seen_ref, sems.at[0]), pltpu.make_async_copy(len_hbm, len_ref, sems.at[1])]
    for load in loads:
        load.start()
    for load in loads:
        load.wait()
    seq_rank = rank_in(SEQ)

    def cached(req):
        return jnp.where(req == 1, len_ref[0], jnp.where(req == 2, len_ref[1], len_ref[2]))

    col = iota((HALF, ROWS), 1)
    base = jnp.where((col & 3) == 0, seen_ref[0], cached(col & 3))
    angles = ((col >> 2) + base).astype(F32) * freq_ref[...]
    cos_ref[...] = jnp.cos(angles)
    sin_ref[...] = jnp.sin(angles)

    def row_ids(shape):
        row = iota(shape, 0)
        return row & 3, (row >> 2) & 7, iota(shape, 1)

    def hidden(see):
        return jnp.where(see, 0.0, MASKED)

    r, t, j = row_ids(hide_long_ref.shape)
    age = (seq_rank * SLOTS + j - seen_ref[0]) & (WIN - 1)
    hide_long_ref[...] = hidden((r == 0) & (age > t))
    r, t, j = row_ids(hide_short_ref.shape)
    hide_short_ref[...] = hidden(((j >> 4) + 1 == r) & (seq_rank * SSLOTS + (j & 15) < cached(r)))
    r, t, j = row_ids(hide_new_ref.shape)
    hide_new_ref[...] = hidden(((j & 3) == r) & ((j >> 2) <= t) & (seq_rank == 0))


def attend_kernel(
    x_ref, gain_ref, cos_ref, sin_ref, hide_long_ref, hide_short_ref, hide_new_ref, wq_ref, wk_ref, wv_ref,
    lk_ref, lv_ref, sk_ref, sv_ref, part_ref, own_ref,
):
    team_rank = rank_in(TEAM)
    x_bf = wide_rows(lambda c: unpack_rows(x_ref[c]))
    x = x_bf.astype(F32)
    mean_square = jnp.mean(x * x, axis=-1, keepdims=True)
    normed = (x * lax.rsqrt(mean_square + EPS) * gain_ref[...].astype(F32).reshape(1, D)).astype(BF16)
    pick = (iota((8, ROWS), 1) == team_rank * TOK + iota((8, ROWS), 0)).astype(BF16)
    own_ref[...] = mm(pick, x_bf, NN)[:TOK]

    cos = cos_ref[...]
    sin = sin_ref[...]

    def rope(v):
        front, back = v[:HALF], v[HALF:]
        return jnp.concatenate([front * cos - back * sin, back * cos + front * sin], axis=0)

    q_t = mm(wq_ref[...], normed, NT)
    k_t = rope(mm(wk_ref[...], normed, NT)).astype(BF16)
    v_t = mm(wv_ref[...], normed, NT).astype(BF16)
    q_all = jnp.concatenate([rope(q_t[h * HD : (h + 1) * HD]) for h in range(GROUP)], axis=1)
    q = q_all.T.astype(BF16)

    scale = 1.0 / math.sqrt(HD)
    n_rows = GROUP * ROWS
    sk = jnp.concatenate([sk_ref[:, r * HD : (r + 1) * HD] for r in range(REQS - 1)], axis=0)
    sv = jnp.concatenate([sv_ref[:, r * HD : (r + 1) * HD] for r in range(REQS - 1)], axis=0)

    def scores(raw, hide_ref):
        hide = hide_ref[...]
        return jnp.where(hide < 0.0, MASKED, raw * scale), hide

    s_long, hide_long = scores(mm(q, lk_ref[...], NN), hide_long_ref)
    s_short, hide_short = scores(mm(q, sk, NT), hide_short_ref)
    s_new, hide_new = scores(mm(q, k_t, NN), hide_new_ref)
    top = jnp.maximum(
        jnp.maximum(jnp.max(s_long, axis=-1, keepdims=True), jnp.max(s_short, axis=-1, keepdims=True)),
        jnp.max(s_new, axis=-1, keepdims=True),
    )
    w_long = jnp.where(hide_long < 0.0, 0.0, jnp.exp(s_long - top))
    w_short = jnp.where(hide_short < 0.0, 0.0, jnp.exp(s_short - top))
    w_new = jnp.where(hide_new < 0.0, 0.0, jnp.exp(s_new - top))
    total = (
        jnp.sum(w_long, axis=-1, keepdims=True)
        + jnp.sum(w_short, axis=-1, keepdims=True)
        + jnp.sum(w_new, axis=-1, keepdims=True)
    )
    acc = (
        mm(w_long.astype(BF16), lv_ref[...], NT)
        + mm(w_short.astype(BF16), sv, NN)
        + mm(w_new.astype(BF16), v_t, NT)
    )
    top_a, top_b, top_c = split3(top)
    sum_a, sum_b, _ = split3(total)
    acc = jnp.concatenate([acc, jnp.zeros((n_rows, 128 - HD), F32)], axis=1)
    lane = iota(acc.shape, 1)
    for k, v in enumerate((top_a, top_b, top_c, sum_a, sum_b)):
        acc = jnp.where(lane == HD + k, v, acc)
    for team in range(NG):
        rows = jnp.concatenate(
            [acc[h * ROWS + team * TOK : h * ROWS + (team + 1) * TOK] for h in range(GROUP)], axis=0
        ).astype(BF16)
        for to in range(NSEQ):
            if team_of(to) == team:
                part_ref[to] = rows


def combine_kernel(part_ref, wo_ref, out_ref):
    part = part_ref[...]
    src = iota((128, 256), 0)
    dst = iota((128, 256), 1)
    spread = (
        ((dst < 128) & (src >= HD) & (src < HD + 3)) | ((dst >= 128) & (src >= HD + 3) & (src < HD + 5))
    ).astype(BF16)
    stats = mm(part.reshape(NSEQ * GROUP * TOK, 128), spread, NN)
    top = stats[:, :128].reshape(NSEQ, GROUP * TOK, 128)
    total = stats[:, 128:].reshape(NSEQ, GROUP * TOK, 128)
    factor = jnp.exp(top - jnp.max(top, axis=0, keepdims=True))
    weighted = jnp.sum(part.astype(F32) * factor, axis=0)
    attended = weighted / jnp.sum(total * factor, axis=0)
    attended = jnp.concatenate([attended[h * TOK : (h + 1) * TOK, :HD] for h in range(GROUP)], axis=1)
    term = mm(attended.astype(BF16), wo_ref[...], NN).astype(BF16)
    for to in range(NTP):
        out_ref[to] = term


def mlp_kernel(part_ref, own_ref, gain_ref, wg_ref, wu_ref, wd_ref, out_ref):
    tp_rank = lax.axis_index("y") * NC + lax.axis_index("c")
    head_sum = jnp.sum(part_ref[...].astype(F32), axis=0)
    stream = own_ref[...] + head_sum
    mean_square = jnp.mean(stream * stream, axis=-1, keepdims=True)
    mlp_in = stream * lax.rsqrt(mean_square + EPS) * gain_ref[...].astype(F32).reshape(1, D)
    mlp_in = jnp.concatenate([mlp_in, jnp.zeros((16 - TOK, D), F32)], axis=0).astype(BF16)
    gate = mm(wg_ref[...], mlp_in, NT)
    up = mm(wu_ref[...], mlp_in, NT)
    hidden = (gate / (1.0 + jnp.exp(-gate)) * up).astype(BF16)
    down = mm(hidden, wd_ref[...], TN)[:TOK]
    for to in range(NTP):
        cols = slice(to * LOCAL, (to + 1) * LOCAL)
        piece = (down[:, cols] + jnp.where(tp_rank == to, head_sum[:, cols], 0.0)).astype(BF16)
        tiles = [piece[p : p + 2, k : k + 128] for p in (0, 2) for k in (0, 128)]
        tiles.append(jnp.concatenate([piece[:2, 256:], piece[2:, 256:]], axis=1))
        for g_to in range(NG):
            for k, tile in enumerate(tiles):
                out_ref[g_to * NTP + to, k] = tile


def call(kernel, out_shape, args, scratch=(), in_hbm=()):
    specs = [pl.BlockSpec(memory_space=pltpu.HBM if i in in_hbm else pltpu.VMEM) for i in range(len(args))]
    return pl.pallas_call(
        kernel,
        out_shape=out_shape,
        in_specs=specs,
        scratch_shapes=scratch,
        cost_estimate=pl.CostEstimate(flops=50_000_000_000, bytes_accessed=100_000_000, transcendentals=0),
        compiler_params=pltpu.CompilerParams(vmem_limit_bytes=16 * 1024 * 1024),
    )(*args)


def body(
    tokens_in, attn_gain, mlp_gain, proj_query, proj_key, proj_value, proj_out, proj_gate, proj_up,
    proj_down, long_keys, long_values, short_keys, short_values, long_seen, short_len,
):
    freq = 10000.0 ** (-2.0 * np.arange(HALF) / HD)
    freq = jnp.asarray(np.repeat(freq[:, None], ROWS, axis=1).astype(np.float32))
    def f32_of(*dims):
        return jax.ShapeDtypeStruct(dims, F32)

    copies, after = call(spread_kernel, (jax.ShapeDtypeStruct((NTP, ROWS * LOCAL // 128, 128), BF16), f32_of(8, 128)), (tokens_in,))
    n_rows = GROUP * ROWS
    tables = call(
        table_kernel,
        (f32_of(HALF, ROWS), f32_of(HALF, ROWS), f32_of(n_rows, SLOTS), f32_of(n_rows, 3 * SSLOTS), f32_of(n_rows, ROWS)),
        (after, long_seen, short_len, freq),
        (pltpu.SMEM((1,), jnp.int32), pltpu.SMEM((3,), jnp.int32), pltpu.SemaphoreType.DMA((2,))),
        {1, 2},
    )
    x_all = lax.all_to_all(copies, TP, 0, 0, tiled=True)
    parts, own = call(
        attend_kernel,
        (jax.ShapeDtypeStruct((NSEQ, GROUP * TOK, 128), BF16), jax.ShapeDtypeStruct((TOK, D), F32)),
        (
            x_all, attn_gain, *tables,
            proj_query.T, proj_key.T, proj_value.T,
            long_keys.reshape(SLOTS, HD).T, long_values.reshape(SLOTS, HD).T,
            short_keys.reshape(SSLOTS, 3 * HD), short_values.reshape(SSLOTS, 3 * HD),
        ),
    )
    parts = lax.all_to_all(parts, SEQ, 0, 0, tiled=True)
    terms = call(combine_kernel, jax.ShapeDtypeStruct((NTP, TOK, D), BF16), (parts, proj_out))
    terms = lax.all_to_all(terms, TP, 0, 0, tiled=True)
    pieces = call(
        mlp_kernel,
        jax.ShapeDtypeStruct((NG * NTP, 5, 2, 128), BF16),
        (terms, own, mlp_gain, proj_gate.T, proj_up.T, proj_down),
    )
    pieces = lax.all_to_all(pieces, TEAM + TP, 0, 0, tiled=True)
    return call(finish_kernel, jax.ShapeDtypeStruct((STEPS, REQS, LOCAL), BF16), (pieces, tokens_in))


def solution(mesh):
    fine = Mesh(mesh.devices.reshape(tuple(SEQ_SIZES.values()) + (NY, NC)), SEQ + TP)
    cols = P(None, TP)
    rows = P(TP, None)
    cache = P(SEQ, TP, None)
    in_specs = (
        P(None, None, TP), P(), P(), cols, cols, cols, rows, cols, cols, rows,
        cache, cache, cache, cache, P(), P(),
    )
    return jax.shard_map(body, mesh=fine, in_specs=in_specs, out_specs=P(None, None, TP), check_vma=False)
```

time: 64 us -> 62.8 us (0.981)
  waiting for transfers between devices: 5.23 us -> 4.1 us
    all_to_all x1, waiting for transfers between devices: 5.23 us -> 4.1 us  [body(): x_all = lax.all_to_all(copies, TP, 0, 0, tiled=True)]
    pallas_call x5 -> x6, Pallas kernels: 6.22 us -> 6.61 us  [call(): pl.pallas_call(kernel, out_shape=out_shape, in_specs=specs, scratch_shape...]
  transfers between devices with their start and end apart: 1 -> 1, of which waited for: 1 -> 1; matrix products, arithmetic and copies ran while one was open for 0% -> 0% of each run, Pallas kernels for 0% -> 1%
where the time goes in v4:
time: 62.8 us; the launch traced here: 62.5 us
  blocking collectives  43.7 us (70%)
  Pallas kernels  6.61 us (11%)
  starting transfers between devices  6.48 us (10%)
  waiting for transfers between devices  4.1 us (7%)
  between operations  0.85 us (1%)
  local copies, waits for them, and re-layouts  0.82 us (1%)
    all_to_all x1, blocking collectives, body(): parts = lax.all_to_all(parts, SEQ, 0, 0, tiled=True)  19.7 us
    all_to_all x1, blocking collectives, body(): pieces = lax.all_to_all(pieces, TEAM + TP, 0, 0, tiled=True)  13.4 us
    all_to_all x1, blocking collectives, body(): terms = lax.all_to_all(terms, TP, 0, 0, tiled=True)  10.6 us
    pallas_call x6, Pallas kernels, call(): pl.pallas_call(kernel, out_shape=out_shape, in_specs=specs, scratch_shape...  6.61 us
    all_to_all x1, starting transfers between devices, body(): x_all = lax.all_to_all(copies, TP, 0, 0, tiled=True)  6.48 us
    all_to_all x1, waiting for transfers between devices, body(): x_all = lax.all_to_all(copies, TP, 0, 0, tiled=True)  4.1 us
  transfers between devices with their start and end apart: 1, of which 1 were waited for; matrix products, arithmetic and copies ran while one was open for 0% of the time, Pallas kernels for 1%

profile of v4, /device:TPU:1, one launch (start us, length us, event | category | flops | bytes accessed | tf_op | source)
XLA Modules:
  0.0 62.5 jit_solution(13601557615615227098)
XLA Ops:
  0.0 0.7 %copy-done.7 = bf16[8,4,320]{2,1,0:T(4,128)(2,1)S(1)} copy-done((bf16[8,4,320]{2,1,0:T(4,128)(2,1)S(1)}, bf16[8,4,320]{2,1,0:T(4,128)(2,1)}, u32[]{:S(2)}) %copy-start.7) | copy-done | bytes 20504
  0.7 0.7 %shard_map.163 = (bf16[8,80,128]{2,1,0:T(8,128)(2,1)}, f32[8,128]{1,0:T(8,128)S(1)}) custom-call(bf16[8,4,320]{2,1,0:T(4,128)(2,1)S(1)} %copy-done.7), custom_call_target="tpu_custom_call" | custom-call | flops 49999998976 | bytes 100000000 | tf_op jit(solution)/shard_map/pallas_call | solution.py:247
  1.5 6.5 %all-to-all-start = ((bf16[8,80,128]{2,1,0:T(8,128)(2,1)}), bf16[8,80,128]{2,1,0:T(8,128)(2,1)S(1)}, u32[]{:S(2)}, u32[]{:S(2)}) async-start(bf16[8,80,128]{2,1,0:T(8,128)(2,1)} %get-tuple-element.14), calls=%async_computation | async-start | bytes 327680 | tf_op jit(solution)/shard_map/all_to_all | solution.py:275
  8.6 0.0 copy-done.15
  8.6 0.0 copy-done.16
  8.6 0.0 copy-start.3
  8.6 0.0 copy-start.5
  8.7 0.0 copy-start.6
  8.7 0.0 copy-start.9
  8.7 0.0 copy-start.10
  8.7 0.0 copy-start.11
  8.7 0.0 copy-start.12
  8.7 0.0 copy-start.13
  8.7 0.7 %shard_map.164 = (f32[40,32]{1,0:T(8,128)S(1)}, f32[40,32]{1,0:T(8,128)S(1)}, f32[128,128]{1,0:T(8,128)S(1)}, f32[128,48]{1,0:T(8,128)S(1)}, f32[128,32]{1,0:T(8,128)S(1)}) custom-call(f32[8,128]{1,0:T(8,128)S(1)} %get-tuple-element.15.after_ref, s32[1]{0:T(128)S(6)} %copy.18.seen_hbm, s32[3]{0:T(128)S(1)} %copy-done.15, f32[40,32]{1,0:T(8,128)S(1)} %copy-done.16), custom_call_target="tpu_custom_call" | custom-call | flops 49999998976 | bytes 100000000 | tf_op jit(solution)/shard_map/pallas_call | solution.py:247
  9.4 4.1 %all-to-all-done.x_ref = bf16[8,80,128]{2,1,0:T(8,128)(2,1)S(1)} async-done(((bf16[8,80,128]{2,1,0:T(8,128)(2,1)}), bf16[8,80,128]{2,1,0:T(8,128)(2,1)S(1)}, u32[]{:S(2)}, u32[]{:S(2)}) %all-to-all-start) | async-done | bytes 163872 | tf_op jit(solution)/shard_map/all_to_all | solution.py:275
  13.5 0.0 copy-done.3
  13.5 0.0 copy-done.5
  13.5 0.0 copy-done.6
  13.5 0.0 copy-done.9
  13.6 0.0 copy-done.10
  13.6 0.0 copy-done.11
  13.6 0.0 copy-start.4
  13.6 1.7 %shard_map.165 = (bf16[32,16,128]{2,1,0:T(8,128)(2,1)S(1)}, f32[4,2560]{1,0:T(4,128)S(1)}) custom-call(bf16[8,80,128]{2,1,0:T(8,128)(2,1)S(1)} %all-to-all-done.x_ref, bf16[2560]{0:T(1024)(128)(2,1)S(1)} %copy-done.13, f32[40,32]{1,0:T(8,128)S(1)} %get-tuple-element.16.cos_ref, f32[40,32]{1,0:T(8,128)S(1)} %get-tuple-element.17.sin_ref, ...), custom_call_target="tpu_custom_call" | custom-call | flops 49999998976 | bytes 100000000 | tf_op jit(solution)/shard_map/pallas_call | solution.py:247
  15.3 19.7 %all_to_all.20.part_ref = bf16[32,16,128]{2,1,0:T(8,128)(2,1)S(1)} all-to-all(bf16[32,16,128]{2,1,0:T(8,128)(2,1)S(1)} %get-tuple-element.21), channel_id=1, replica_groups=mesh['zh'=4,'zl'=2,'xh'=2,'xl'=2,'y'=4,'c'=2] {'zh','zl','xh','xl'}, dimensions={0} | all-to-all | bytes 262144 | tf_op jit(solution)/shard_map/all_to_all | solution.py:286
  35.0 0.0 copy-start.14
  35.0 0.8 %shard_map.166 = bf16[8,4,2560]{2,1,0:T(4,128)(2,1)S(1)} custom-call(bf16[32,16,128]{2,1,0:T(8,128)(2,1)S(1)} %all_to_all.20.part_ref, bf16[320,2560]{1,0:T(8,128)(2,1)S(1)} %copy-done.4), custom_call_target="tpu_custom_call" | custom-call | flops 49999998976 | bytes 100000000 | tf_op jit(solution)/shard_map/pallas_call | solution.py:247
  35.7 10.6 %all_to_all.21.part_ref = bf16[8,4,2560]{2,1,0:T(4,128)(2,1)S(1)} all-to-all(bf16[8,4,2560]{2,1,0:T(4,128)(2,1)S(1)} %shard_map.166), channel_id=1, replica_groups=mesh['zh'=4,'zl'=2,'xh'=2,'xl'=2,'y'=4,'c'=2] {'y','c'}, dimensions={0} | all-to-all | bytes 327680 | tf_op jit(solution)/shard_map/all_to_all | solution.py:288
  46.3 0.0 copy-done.1
  46.3 0.0 copy-start.8
  46.3 2.0 %shard_map.167 = bf16[64,5,2,128]{3,2,1,0:T(2,128)(2,1)S(1)} custom-call(bf16[8,4,2560]{2,1,0:T(4,128)(2,1)S(1)} %all_to_all.21.part_ref, f32[4,2560]{1,0:T(4,128)S(1)} %get-tuple-element.22.own_ref, bf16[2560]{0:T(1024)(128)(2,1)S(1)} %copy-done.14, bf16[432,2560]{1,0:T(8,128)(2,1)S(1)} %bitcast.13, bf16[432,2560]{1,0:T(8,128)(2,1)S(1)} %bitcast.14, ...), custom_call_target="tpu_custom_call" | custom-call | flops 49999998976 | bytes 100000000 | tf_op jit(solution)/shard_map/pallas_call | solution.py:247
  48.3 13.4 %all_to_all.22.piece_ref = bf16[64,5,2,128]{3,2,1,0:T(2,128)(2,1)S(1)} all-to-all(bf16[64,5,2,128]{3,2,1,0:T(2,128)(2,1)S(1)} %shard_map.167), channel_id=1, replica_groups=mesh['zh'=4,'zl'=2,'xh'=2,'xl'=2,'y'=4,'c'=2] {'zl','xh','xl','y','c'}, dimensions={0} | all-to-all | bytes 327680 | tf_op jit(solution)/shard_map/all_to_all | solution.py:294
  61.8 0.8 %shard_map.168 = bf16[8,4,320]{2,1,0:T(4,128)(2,1)} custom-call(bf16[64,5,2,128]{3,2,1,0:T(2,128)(2,1)S(1)} %all_to_all.22.piece_ref, bf16[8,4,320]{2,1,0:T(4,128)(2,1)S(1)} %copy-done.8), custom_call_target="tpu_custom_call" | custom-call | flops 49999998976 | bytes 100000000 | tf_op jit(solution)/shard_map/pallas_call | solution.py:247
  (13 shorter events, 0.0 us)
Async XLA Ops:
  0.0 0.7 %copy-start.7 = (bf16[8,4,320]{2,1,0:T(4,128)(2,1)S(1)}, bf16[8,4,320]{2,1,0:T(4,128)(2,1)}, u32[]{:S(2)}) copy-start(bf16[8,4,320]{2,1,0:T(4,128)(2,1)} %tokens_ref.3) | copy-start | bytes 61444
  0.7 7.9 %copy-start.15 = (s32[3]{0:T(128)S(1)}, s32[3]{0:T(128)}, u32[]{:S(2)}) copy-start(s32[3]{0:T(128)} %len_hbm.1) | copy-start | bytes 40
  0.7 7.9 %copy-start.16 = (f32[40,32]{1,0:T(8,128)S(1)}, f32[40,32]{1,0:T(8,128)}, u32[]{:S(2)}) copy-start(f32[40,32]{1,0:T(8,128)} %constant.2.clone.freq_ref) | copy-start | bytes 15364
  1.5 12.1 %all-to-all-start = ((bf16[8,80,128]{2,1,0:T(8,128)(2,1)}), bf16[8,80,128]{2,1,0:T(8,128)(2,1)S(1)}, u32[]{:S(2)}, u32[]{:S(2)}) async-start(bf16[8,80,128]{2,1,0:T(8,128)(2,1)} %get-tuple-element.14), calls=%async_computation | async-start | bytes 327680 | tf_op jit(solution)/shard_map/all_to_all | solution.py:275
  8.6 4.9 %copy-start.3 = (bf16[2560,320]{0,1:T(8,128)(2,1)S(1)}, bf16[2560,320]{0,1:T(8,128)(2,1)}, u32[]{:S(2)}) copy-start(bf16[2560,320]{0,1:T(8,128)(2,1)} %param.20) | copy-start | bytes 4915204
  8.6 4.9 %copy-start.5 = (bf16[2560,80]{0,1:T(8,128)(2,1)S(1)}, bf16[2560,80]{0,1:T(8,128)(2,1)}, u32[]{:S(2)}) copy-start(bf16[2560,80]{0,1:T(8,128)(2,1)} %param.21) | copy-start | bytes 1228804
  8.7 4.9 %copy-start.6 = (bf16[2560,80]{0,1:T(8,128)(2,1)S(1)}, bf16[2560,80]{0,1:T(8,128)(2,1)}, u32[]{:S(2)}) copy-start(bf16[2560,80]{0,1:T(8,128)(2,1)} %param.22) | copy-start | bytes 1228804
  8.7 4.9 %copy-start.9 = (bf16[128,1,80]{0,2,1:T(8,128)(2,1)S(1)}, bf16[128,1,80]{0,2,1:T(8,128)(2,1)}, u32[]{:S(2)}) copy-start(bf16[128,1,80]{0,2,1:T(8,128)(2,1)} %param.27) | copy-start | bytes 61444
  8.7 4.9 %copy-start.10 = (bf16[128,1,80]{0,2,1:T(8,128)(2,1)S(1)}, bf16[128,1,80]{0,2,1:T(8,128)(2,1)}, u32[]{:S(2)}) copy-start(bf16[128,1,80]{0,2,1:T(8,128)(2,1)} %param.28) | copy-start | bytes 61444
  8.7 4.9 %copy-start.11 = (bf16[16,1,240]{2,0,1:T(8,128)(2,1)S(1)}, bf16[16,1,240]{2,0,1:T(8,128)(2,1)}, u32[]{:S(2)}) copy-start(bf16[16,1,240]{2,0,1:T(8,128)(2,1)} %param.29) | copy-start | bytes 23044
  8.7 4.9 %copy-start.12 = (bf16[16,1,240]{2,0,1:T(8,128)(2,1)S(1)}, bf16[16,1,240]{2,0,1:T(8,128)(2,1)}, u32[]{:S(2)}) copy-start(bf16[16,1,240]{2,0,1:T(8,128)(2,1)} %param.30) | copy-start | bytes 23044
  8.7 4.9 %copy-start.13 = (bf16[2560]{0:T(1024)(128)(2,1)S(1)}, bf16[2560]{0:T(1024)(128)(2,1)}, u32[]{:S(2)}) copy-start(bf16[2560]{0:T(1024)(128)(2,1)} %gain_ref.2) | copy-start | bytes 15364
  13.6 21.3 %copy-start.4 = (bf16[320,2560]{1,0:T(8,128)(2,1)S(1)}, bf16[320,2560]{1,0:T(8,128)(2,1)}, u32[]{:S(2)}) copy-start(bf16[320,2560]{1,0:T(8,128)(2,1)} %wo_ref.1) | copy-start | bytes 4915204
  34.9 11.4 %copy-start = (bf16[2560,432]{0,1:T(8,128)(2,1)S(1)}, bf16[2560,432]{0,1:T(8,128)(2,1)}, u32[]{:S(2)}) copy-start(bf16[2560,432]{0,1:T(8,128)(2,1)} %param.24) | copy-start | bytes 6635524
  34.9 11.4 %copy-start.1 = (bf16[2560,432]{0,1:T(8,128)(2,1)S(1)}, bf16[2560,432]{0,1:T(8,128)(2,1)}, u32[]{:S(2)}) copy-start(bf16[2560,432]{0,1:T(8,128)(2,1)} %param.25) | copy-start | bytes 6635524
  34.9 11.4 %copy-start.2 = (bf16[432,2560]{1,0:T(8,128)(2,1)S(1)}, bf16[432,2560]{1,0:T(8,128)(2,1)}, u32[]{:S(2)}) copy-start(bf16[432,2560]{1,0:T(8,128)(2,1)} %wd_ref.1) | copy-start | bytes 6635524
  35.0 11.4 %copy-start.14 = (bf16[2560]{0:T(1024)(128)(2,1)S(1)}, bf16[2560]{0:T(1024)(128)(2,1)}, u32[]{:S(2)}) copy-start(bf16[2560]{0:T(1024)(128)(2,1)} %gain_ref.3) | copy-start | bytes 15364
  46.3 15.4 %copy-start.8 = (bf16[8,4,320]{2,1,0:T(4,128)(2,1)S(1)}, bf16[8,4,320]{2,1,0:T(4,128)(2,1)}, u32[]{:S(2)}) copy-start(bf16[8,4,320]{2,1,0:T(4,128)(2,1)} %tokens_ref.3) | copy-start | bytes 61444

commit v5 on v4

--- a/solution.py
+++ b/solution.py
@@ -29,6 +29,7 @@
 LOCAL = D // NTP
 SLOTS = WIN // NSEQ
 SSLOTS = 16
+HELD = SLOTS + 3 * SSLOTS
 EPS = 1e-05
 MASKED = -1e30
 TP = ("y", "c")
@@ -99,7 +100,8 @@
 
 
 def table_kernel(
-    after_ref, seen_hbm, len_hbm, freq_ref, cos_ref, sin_ref, hide_long_ref, hide_short_ref, hide_new_ref, seen_ref, len_ref, sems,
+    after_ref, seen_hbm, len_hbm, freq_ref, lk_ref, lv_ref, sk_ref, sv_ref,
+    cos_ref, sin_ref, hide_ref, keys_ref, values_ref, seen_ref, len_ref, sems,
 ):
     loads = [pltpu.make_async_copy(seen_hbm, seen_ref, sems.at[0]), pltpu.make_async_copy(len_hbm, len_ref, sems.at[1])]
     for load in loads:
@@ -117,25 +119,24 @@
     cos_ref[...] = jnp.cos(angles)
     sin_ref[...] = jnp.sin(angles)
 
-    def row_ids(shape):
-        row = iota(shape, 0)
-        return row & 3, (row >> 2) & 7, iota(shape, 1)
-
-    def hidden(see):
-        return jnp.where(see, 0.0, MASKED)
-
-    r, t, j = row_ids(hide_long_ref.shape)
-    age = (seq_rank * SLOTS + j - seen_ref[0]) & (WIN - 1)
-    hide_long_ref[...] = hidden((r == 0) & (age > t))
-    r, t, j = row_ids(hide_short_ref.shape)
-    hide_short_ref[...] = hidden(((j >> 4) + 1 == r) & (seq_rank * SSLOTS + (j & 15) < cached(r)))
-    r, t, j = row_ids(hide_new_ref.shape)
-    hide_new_ref[...] = hidden(((j & 3) == r) & ((j >> 2) <= t) & (seq_rank == 0))
+    def hide(first, count, see):
+        shape = (count, GROUP * ROWS)
+        lane = iota(shape, 1)
+        hide_ref[first : first + count] = jnp.where(see(lane & 3, (lane >> 2) & 7, iota(shape, 0)), 0.0, MASKED)
+
+    hide(0, SLOTS, lambda r, t, j: (r == 0) & (((seq_rank * SLOTS + j - seen_ref[0]) & (WIN - 1)) > t))
+    hide(SLOTS, 3 * SSLOTS, lambda r, t, j: ((j >> 4) + 1 == r) & (seq_rank * SSLOTS + (j & 15) < cached(r)))
+    hide(HELD, ROWS, lambda r, t, j: ((j & 3) == r) & ((j >> 2) <= t) & (seq_rank == 0))
+    keys_ref[:SLOTS] = lk_ref[...].astype(F32).T.astype(BF16)
+    for req in range(REQS - 1):
+        cols = slice(req * HD, (req + 1) * HD)
+        keys_ref[SLOTS + req * SSLOTS : SLOTS + (req + 1) * SSLOTS] = sk_ref[:, cols]
+    short = jnp.concatenate([sv_ref[:, r * HD : (r + 1) * HD].astype(F32) for r in range(REQS - 1)], axis=0)
+    values_ref[...] = jnp.concatenate([lv_ref[...].astype(F32), short.T], axis=1).astype(BF16)
 
 
 def attend_kernel(
-    x_ref, gain_ref, cos_ref, sin_ref, hide_long_ref, hide_short_ref, hide_new_ref, wq_ref, wk_ref, wv_ref,
-    lk_ref, lv_ref, sk_ref, sv_ref, part_ref, own_ref,
+    x_ref, gain_ref, cos_ref, sin_ref, hide_ref, keys_ref, values_ref, wq_ref, wk_ref, wv_ref, part_ref, own_ref,
 ):
     team_rank = rank_in(TEAM)
     x_bf = wide_rows(lambda c: unpack_rows(x_ref[c]))
@@ -152,47 +153,23 @@
         front, back = v[:HALF], v[HALF:]
         return jnp.concatenate([front * cos - back * sin, back * cos + front * sin], axis=0)
 
-    q_t = mm(wq_ref[...], normed, NT)
-    k_t = rope(mm(wk_ref[...], normed, NT)).astype(BF16)
-    v_t = mm(wv_ref[...], normed, NT).astype(BF16)
-    q_all = jnp.concatenate([rope(q_t[h * HD : (h + 1) * HD]) for h in range(GROUP)], axis=1)
-    q = q_all.T.astype(BF16)
-
-    scale = 1.0 / math.sqrt(HD)
-    n_rows = GROUP * ROWS
-    sk = jnp.concatenate([sk_ref[:, r * HD : (r + 1) * HD] for r in range(REQS - 1)], axis=0)
-    sv = jnp.concatenate([sv_ref[:, r * HD : (r + 1) * HD] for r in range(REQS - 1)], axis=0)
-
-    def scores(raw, hide_ref):
-        hide = hide_ref[...]
-        return jnp.where(hide < 0.0, MASKED, raw * scale), hide
-
-    s_long, hide_long = scores(mm(q, lk_ref[...], NN), hide_long_ref)
-    s_short, hide_short = scores(mm(q, sk, NT), hide_short_ref)
-    s_new, hide_new = scores(mm(q, k_t, NN), hide_new_ref)
-    top = jnp.maximum(
-        jnp.maximum(jnp.max(s_long, axis=-1, keepdims=True), jnp.max(s_short, axis=-1, keepdims=True)),
-        jnp.max(s_new, axis=-1, keepdims=True),
-    )
-    w_long = jnp.where(hide_long < 0.0, 0.0, jnp.exp(s_long - top))
-    w_short = jnp.where(hide_short < 0.0, 0.0, jnp.exp(s_short - top))
-    w_new = jnp.where(hide_new < 0.0, 0.0, jnp.exp(s_new - top))
-    total = (
-        jnp.sum(w_long, axis=-1, keepdims=True)
-        + jnp.sum(w_short, axis=-1, keepdims=True)
-        + jnp.sum(w_new, axis=-1, keepdims=True)
-    )
-    acc = (
-        mm(w_long.astype(BF16), lv_ref[...], NT)
-        + mm(w_short.astype(BF16), sv, NN)
-        + mm(w_new.astype(BF16), v_t, NT)
-    )
-    top_a, top_b, top_c = split3(top)
-    sum_a, sum_b, _ = split3(total)
-    acc = jnp.concatenate([acc, jnp.zeros((n_rows, 128 - HD), F32)], axis=1)
-    lane = iota(acc.shape, 1)
-    for k, v in enumerate((top_a, top_b, top_c, sum_a, sum_b)):
-        acc = jnp.where(lane == HD + k, v, acc)
+    k_new = rope(mm(wk_ref[...], normed, NT)).T.astype(BF16)
+    v_new = mm(wv_ref[...], normed, NT).astype(BF16)
+    q_t = mm(normed, wq_ref[...], NT).T
+    q = jnp.concatenate([rope(q_t[h * HD : (h + 1) * HD]) for h in range(GROUP)], axis=1).astype(BF16)
+
+    seen = hide_ref[...] == 0.0
+    scores = mm(jnp.concatenate([keys_ref[...], k_new], axis=0), q, NN) * (1.0 / math.sqrt(HD))
+    scores = jnp.where(seen, scores, MASKED)
+    top = jnp.max(scores, axis=0, keepdims=True)
+    weights = jnp.where(seen, jnp.exp(scores - top), 0.0)
+    total = jnp.sum(weights, axis=0, keepdims=True)
+    weights = weights.astype(BF16)
+    acc = mm(values_ref[...], weights[:HELD], NN) + mm(v_new, weights[HELD:], NN)
+    some = total > 0.0
+    level = jnp.where(some, top + jnp.log(jnp.where(some, total, 1.0)), MASKED)
+    filler = jnp.zeros((128 - HD - 3, GROUP * ROWS), F32)
+    acc = jnp.concatenate([acc * (1.0 / jnp.where(some, total, 1.0)), *split3(level), filler], axis=0).T
     for team in range(NG):
         rows = jnp.concatenate(
             [acc[h * ROWS + team * TOK : h * ROWS + (team + 1) * TOK] for h in range(GROUP)], axis=0
@@ -204,17 +181,11 @@
 
 def combine_kernel(part_ref, wo_ref, out_ref):
     part = part_ref[...]
-    src = iota((128, 256), 0)
-    dst = iota((128, 256), 1)
-    spread = (
-        ((dst < 128) & (src >= HD) & (src < HD + 3)) | ((dst >= 128) & (src >= HD + 3) & (src < HD + 5))
-    ).astype(BF16)
-    stats = mm(part.reshape(NSEQ * GROUP * TOK, 128), spread, NN)
-    top = stats[:, :128].reshape(NSEQ, GROUP * TOK, 128)
-    total = stats[:, 128:].reshape(NSEQ, GROUP * TOK, 128)
-    factor = jnp.exp(top - jnp.max(top, axis=0, keepdims=True))
-    weighted = jnp.sum(part.astype(F32) * factor, axis=0)
-    attended = weighted / jnp.sum(total * factor, axis=0)
+    src = iota((128, 128), 0)
+    spread = ((src >= HD) & (src < HD + 3)).astype(BF16)
+    level = mm(part.reshape(NSEQ * GROUP * TOK, 128), spread, NN).reshape(NSEQ, GROUP * TOK, 128)
+    factor = jnp.exp(level - jnp.max(level, axis=0, keepdims=True))
+    attended = jnp.sum(part.astype(F32) * factor, axis=0) / jnp.sum(factor, axis=0)
     attended = jnp.concatenate([attended[h * TOK : (h + 1) * TOK, :HD] for h in range(GROUP)], axis=1)
     term = mm(attended.astype(BF16), wo_ref[...], NN).astype(BF16)
     for to in range(NTP):
@@ -228,10 +199,10 @@
     mean_square = jnp.mean(stream * stream, axis=-1, keepdims=True)
     mlp_in = stream * lax.rsqrt(mean_square + EPS) * gain_ref[...].astype(F32).reshape(1, D)
     mlp_in = jnp.concatenate([mlp_in, jnp.zeros((16 - TOK, D), F32)], axis=0).astype(BF16)
-    gate = mm(wg_ref[...], mlp_in, NT)
-    up = mm(wu_ref[...], mlp_in, NT)
+    gate = mm(mlp_in, wg_ref[...], NT)
+    up = mm(mlp_in, wu_ref[...], NT)
     hidden = (gate / (1.0 + jnp.exp(-gate)) * up).astype(BF16)
-    down = mm(hidden, wd_ref[...], TN)[:TOK]
+    down = mm(hidden, wd_ref[...], NN)[:TOK]
     for to in range(NTP):
         cols = slice(to * LOCAL, (to + 1) * LOCAL)
         piece = (down[:, cols] + jnp.where(tp_rank == to, head_sum[:, cols], 0.0)).astype(BF16)
@@ -267,8 +238,15 @@
     n_rows = GROUP * ROWS
     tables = call(
         table_kernel,
-        (f32_of(HALF, ROWS), f32_of(HALF, ROWS), f32_of(n_rows, SLOTS), f32_of(n_rows, 3 * SSLOTS), f32_of(n_rows, ROWS)),
-        (after, long_seen, short_len, freq),
+        (
+            f32_of(HALF, ROWS), f32_of(HALF, ROWS), f32_of(HELD + ROWS, n_rows),
+            jax.ShapeDtypeStruct((HELD, HD), BF16), jax.ShapeDtypeStruct((HD, HELD), BF16),
+        ),
+        (
+            after, long_seen, short_len, freq,
+            long_keys.reshape(SLOTS, HD).T, long_values.reshape(SLOTS, HD).T,
+            short_keys.reshape(SSLOTS, 3 * HD), short_values.reshape(SSLOTS, 3 * HD),
+        ),
         (pltpu.SMEM((1,), jnp.int32), pltpu.SMEM((3,), jnp.int32), pltpu.SemaphoreType.DMA((2,))),
         {1, 2},
     )
@@ -277,10 +255,7 @@
         attend_kernel,
         (jax.ShapeDtypeStruct((NSEQ, GROUP * TOK, 128), BF16), jax.ShapeDtypeStruct((TOK, D), F32)),
         (
-            x_all, attn_gain, *tables,
-            proj_query.T, proj_key.T, proj_value.T,
-            long_keys.reshape(SLOTS, HD).T, long_values.reshape(SLOTS, HD).T,
-            short_keys.reshape(SSLOTS, 3 * HD), short_values.reshape(SSLOTS, 3 * HD),
+            x_all, attn_gain, *tables, proj_query.T, proj_key.T, proj_value.T,
         ),
     )
     parts = lax.all_to_all(parts, SEQ, 0, 0, tiled=True)

time: 62.8 us -> 62.6 us (level)
  no operation moved by 1% of the time
where the time goes in v5:
time: 62.6 us; the launch traced here: 62.3 us
  blocking collectives  43.6 us (70%)
  starting transfers between devices  6.48 us (10%)
  Pallas kernels  6.43 us (10%)
  waiting for transfers between devices  4.08 us (7%)
  between operations  0.84 us (1%)
  local copies, waits for them, and re-layouts  0.82 us (1%)
    all_to_all x1, blocking collectives, body(): parts = lax.all_to_all(parts, SEQ, 0, 0, tiled=True)  19.6 us
    all_to_all x1, blocking collectives, body(): pieces = lax.all_to_all(pieces, TEAM + TP, 0, 0, tiled=True)  13.4 us
    all_to_all x1, blocking collectives, body(): terms = lax.all_to_all(terms, TP, 0, 0, tiled=True)  10.6 us
    all_to_all x1, starting transfers between devices, body(): x_all = lax.all_to_all(copies, TP, 0, 0, tiled=True)  6.48 us
    pallas_call x6, Pallas kernels, call(): pl.pallas_call(kernel, out_shape=out_shape, in_specs=specs, scratch_shape...  6.43 us
    all_to_all x1, waiting for transfers between devices, body(): x_all = lax.all_to_all(copies, TP, 0, 0, tiled=True)  4.08 us
  transfers between devices with their start and end apart: 1, of which 1 were waited for; matrix products, arithmetic and copies ran while one was open for 0% of the time, Pallas kernels for 1%

profile of v5, /device:TPU:1, one launch (start us, length us, event | category | flops | bytes accessed | tf_op | source)
XLA Modules:
  0.0 62.3 jit_solution(14913973059905507014)
XLA Ops:
  0.0 0.7 %copy-done.7 = bf16[8,4,320]{2,1,0:T(4,128)(2,1)S(1)} copy-done((bf16[8,4,320]{2,1,0:T(4,128)(2,1)S(1)}, bf16[8,4,320]{2,1,0:T(4,128)(2,1)}, u32[]{:S(2)}) %copy-start.7) | copy-done | bytes 20504
  0.7 0.0 copy-start.15
  0.8 0.0 copy-start.16
  0.8 0.7 %shard_map.163 = (bf16[8,80,128]{2,1,0:T(8,128)(2,1)}, f32[8,128]{1,0:T(8,128)S(1)}) custom-call(bf16[8,4,320]{2,1,0:T(4,128)(2,1)S(1)} %copy-done.7), custom_call_target="tpu_custom_call" | custom-call | flops 49999998976 | bytes 100000000 | tf_op jit(solution)/shard_map/pallas_call | solution.py:218
  1.5 6.5 %all-to-all-start = ((bf16[8,80,128]{2,1,0:T(8,128)(2,1)}), bf16[8,80,128]{2,1,0:T(8,128)(2,1)S(1)}, u32[]{:S(2)}, u32[]{:S(2)}) async-start(bf16[8,80,128]{2,1,0:T(8,128)(2,1)} %get-tuple-element.14), calls=%async_computation | async-start | bytes 327680 | tf_op jit(solution)/shard_map/all_to_all | solution.py:253
  8.6 0.0 copy-done.9
  8.7 0.0 copy-done.10
  8.7 0.0 copy-done.11
  8.7 0.0 copy-done.12
  8.7 0.0 copy-done.15
  8.7 0.0 copy-done.16
  8.7 0.0 copy-start.3
  8.7 0.0 copy-start.5
  8.7 0.0 copy-start.6
  8.7 0.0 copy-start.13
  8.8 0.7 %shard_map.164 = (f32[40,32]{1,0:T(8,128)S(1)}, f32[40,32]{1,0:T(8,128)S(1)}, f32[208,128]{1,0:T(8,128)S(1)}, bf16[176,80]{1,0:T(8,128)(2,1)S(1)}, bf16[80,176]{1,0:T(8,128)(2,1)S(1)}) custom-call(f32[8,128]{1,0:T(8,128)S(1)} %get-tuple-element.15.after_ref, s32[1]{0:T(128)S(6)} %copy.18.seen_hbm, s32[3]{0:T(128)S(1)} %copy-done.15, ...), custom_call_target="tpu_custom_call" | custom-call | flops 49999998976 | bytes 100000000 | tf_op jit(solution)/shard_map/pallas_call | solution.py:218
  9.5 4.1 %all-to-all-done.x_ref = bf16[8,80,128]{2,1,0:T(8,128)(2,1)S(1)} async-done(((bf16[8,80,128]{2,1,0:T(8,128)(2,1)}), bf16[8,80,128]{2,1,0:T(8,128)(2,1)S(1)}, u32[]{:S(2)}, u32[]{:S(2)}) %all-to-all-start) | async-done | bytes 163872 | tf_op jit(solution)/shard_map/all_to_all | solution.py:253
  13.6 0.0 copy-done.3
  13.6 0.0 copy-done.5
  13.6 0.0 copy-done.6
  13.6 0.0 copy-done.13
  13.6 0.0 copy-start.4
  13.6 1.7 %shard_map.165 = (bf16[32,16,128]{2,1,0:T(8,128)(2,1)S(1)}, f32[4,2560]{1,0:T(4,128)S(1)}) custom-call(bf16[8,80,128]{2,1,0:T(8,128)(2,1)S(1)} %all-to-all-done.x_ref, bf16[2560]{0:T(1024)(128)(2,1)S(1)} %copy-done.13, f32[40,32]{1,0:T(8,128)S(1)} %get-tuple-element.16.cos_ref, f32[40,32]{1,0:T(8,128)S(1)} %get-tuple-element.17.sin_ref, ...), custom_call_target="tpu_custom_call" | custom-call | flops 49999998976 | bytes 100000000 | tf_op jit(solution)/shard_map/pallas_call | solution.py:218
  15.3 19.6 %all_to_all.20.part_ref = bf16[32,16,128]{2,1,0:T(8,128)(2,1)S(1)} all-to-all(bf16[32,16,128]{2,1,0:T(8,128)(2,1)S(1)} %get-tuple-element.21), channel_id=1, replica_groups=mesh['zh'=4,'zl'=2,'xh'=2,'xl'=2,'y'=4,'c'=2] {'zh','zl','xh','xl'}, dimensions={0} | all-to-all | bytes 262144 | tf_op jit(solution)/shard_map/all_to_all | solution.py:261
  35.0 0.0 copy-done.4
  35.0 0.0 copy-start.14
  35.0 0.7 %shard_map.166 = bf16[8,4,2560]{2,1,0:T(4,128)(2,1)S(1)} custom-call(bf16[32,16,128]{2,1,0:T(8,128)(2,1)S(1)} %all_to_all.20.part_ref, bf16[320,2560]{1,0:T(8,128)(2,1)S(1)} %copy-done.4), custom_call_target="tpu_custom_call" | custom-call | flops 49999998976 | bytes 100000000 | tf_op jit(solution)/shard_map/pallas_call | solution.py:218
  35.7 10.6 %all_to_all.21.part_ref = bf16[8,4,2560]{2,1,0:T(4,128)(2,1)S(1)} all-to-all(bf16[8,4,2560]{2,1,0:T(4,128)(2,1)S(1)} %shard_map.166), channel_id=1, replica_groups=mesh['zh'=4,'zl'=2,'xh'=2,'xl'=2,'y'=4,'c'=2] {'y','c'}, dimensions={0} | all-to-all | bytes 327680 | tf_op jit(solution)/shard_map/all_to_all | solution.py:263
  46.2 0.0 copy-start.8
  46.3 1.8 %shard_map.167 = bf16[64,5,2,128]{3,2,1,0:T(2,128)(2,1)S(1)} custom-call(bf16[8,4,2560]{2,1,0:T(4,128)(2,1)S(1)} %all_to_all.21.part_ref, f32[4,2560]{1,0:T(4,128)S(1)} %get-tuple-element.22.own_ref, bf16[2560]{0:T(1024)(128)(2,1)S(1)} %copy-done.14, bf16[432,2560]{1,0:T(8,128)(2,1)S(1)} %bitcast.13, bf16[432,2560]{1,0:T(8,128)(2,1)S(1)} %bitcast.14, ...), custom_call_target="tpu_custom_call" | custom-call | flops 49999998976 | bytes 100000000 | tf_op jit(solution)/shard_map/pallas_call | solution.py:218
  48.1 13.4 %all_to_all.22.piece_ref = bf16[64,5,2,128]{3,2,1,0:T(2,128)(2,1)S(1)} all-to-all(bf16[64,5,2,128]{3,2,1,0:T(2,128)(2,1)S(1)} %shard_map.167), channel_id=1, replica_groups=mesh['zh'=4,'zl'=2,'xh'=2,'xl'=2,'y'=4,'c'=2] {'zl','xh','xl','y','c'}, dimensions={0} | all-to-all | bytes 327680 | tf_op jit(solution)/shard_map/all_to_all | solution.py:269
  61.5 0.8 %shard_map.168 = bf16[8,4,320]{2,1,0:T(4,128)(2,1)} custom-call(bf16[64,5,2,128]{3,2,1,0:T(2,128)(2,1)S(1)} %all_to_all.22.piece_ref, bf16[8,4,320]{2,1,0:T(4,128)(2,1)S(1)} %copy-done.8), custom_call_target="tpu_custom_call" | custom-call | flops 49999998976 | bytes 100000000 | tf_op jit(solution)/shard_map/pallas_call | solution.py:218
  (13 shorter events, 0.0 us)
Async XLA Ops:
  0.0 0.7 %copy-start.7 = (bf16[8,4,320]{2,1,0:T(4,128)(2,1)S(1)}, bf16[8,4,320]{2,1,0:T(4,128)(2,1)}, u32[]{:S(2)}) copy-start(bf16[8,4,320]{2,1,0:T(4,128)(2,1)} %tokens_ref.3) | copy-start | bytes 61444
  0.7 7.9 %copy-start.9 = (bf16[128,1,80]{0,2,1:T(8,128)(2,1)S(1)}, bf16[128,1,80]{0,2,1:T(8,128)(2,1)}, u32[]{:S(2)}) copy-start(bf16[128,1,80]{0,2,1:T(8,128)(2,1)} %param.27) | copy-start | bytes 61444
  0.7 7.9 %copy-start.10 = (bf16[128,1,80]{0,2,1:T(8,128)(2,1)S(1)}, bf16[128,1,80]{0,2,1:T(8,128)(2,1)}, u32[]{:S(2)}) copy-start(bf16[128,1,80]{0,2,1:T(8,128)(2,1)} %param.28) | copy-start | bytes 61444
  0.7 7.9 %copy-start.11 = (bf16[16,1,240]{2,0,1:T(8,128)(2,1)S(1)}, bf16[16,1,240]{2,0,1:T(8,128)(2,1)}, u32[]{:S(2)}) copy-start(bf16[16,1,240]{2,0,1:T(8,128)(2,1)} %param.29) | copy-start | bytes 23044
  0.7 7.9 %copy-start.12 = (bf16[16,1,240]{2,0,1:T(8,128)(2,1)S(1)}, bf16[16,1,240]{2,0,1:T(8,128)(2,1)}, u32[]{:S(2)}) copy-start(bf16[16,1,240]{2,0,1:T(8,128)(2,1)} %param.30) | copy-start | bytes 23044
  0.7 7.9 %copy-start.15 = (s32[3]{0:T(128)S(1)}, s32[3]{0:T(128)}, u32[]{:S(2)}) copy-start(s32[3]{0:T(128)} %len_hbm.1) | copy-start | bytes 40
  0.8 7.9 %copy-start.16 = (f32[40,32]{1,0:T(8,128)S(1)}, f32[40,32]{1,0:T(8,128)}, u32[]{:S(2)}) copy-start(f32[40,32]{1,0:T(8,128)} %constant.2.clone.freq_ref) | copy-start | bytes 15364
  1.5 12.1 %all-to-all-start = ((bf16[8,80,128]{2,1,0:T(8,128)(2,1)}), bf16[8,80,128]{2,1,0:T(8,128)(2,1)S(1)}, u32[]{:S(2)}, u32[]{:S(2)}) async-start(bf16[8,80,128]{2,1,0:T(8,128)(2,1)} %get-tuple-element.14), calls=%async_computation | async-start | bytes 327680 | tf_op jit(solution)/shard_map/all_to_all | solution.py:253
  8.7 4.9 %copy-start.3 = (bf16[2560,320]{0,1:T(8,128)(2,1)S(1)}, bf16[2560,320]{0,1:T(8,128)(2,1)}, u32[]{:S(2)}) copy-start(bf16[2560,320]{0,1:T(8,128)(2,1)} %param.20) | copy-start | bytes 4915204
  8.7 4.9 %copy-start.5 = (bf16[2560,80]{0,1:T(8,128)(2,1)S(1)}, bf16[2560,80]{0,1:T(8,128)(2,1)}, u32[]{:S(2)}) copy-start(bf16[2560,80]{0,1:T(8,128)(2,1)} %param.21) | copy-start | bytes 1228804
  8.7 4.8 %copy-start.6 = (bf16[2560,80]{0,1:T(8,128)(2,1)S(1)}, bf16[2560,80]{0,1:T(8,128)(2,1)}, u32[]{:S(2)}) copy-start(bf16[2560,80]{0,1:T(8,128)(2,1)} %param.22) | copy-start | bytes 1228804
  8.7 4.8 %copy-start.13 = (bf16[2560]{0:T(1024)(128)(2,1)S(1)}, bf16[2560]{0:T(1024)(128)(2,1)}, u32[]{:S(2)}) copy-start(bf16[2560]{0:T(1024)(128)(2,1)} %gain_ref.2) | copy-start | bytes 15364
  13.6 21.4 %copy-start.4 = (bf16[320,2560]{1,0:T(8,128)(2,1)S(1)}, bf16[320,2560]{1,0:T(8,128)(2,1)}, u32[]{:S(2)}) copy-start(bf16[320,2560]{1,0:T(8,128)(2,1)} %wo_ref.1) | copy-start | bytes 4915204
  35.0 11.3 %copy-start = (bf16[2560,432]{0,1:T(8,128)(2,1)S(1)}, bf16[2560,432]{0,1:T(8,128)(2,1)}, u32[]{:S(2)}) copy-start(bf16[2560,432]{0,1:T(8,128)(2,1)} %param.24) | copy-start | bytes 6635524
  35.0 11.3 %copy-start.1 = (bf16[2560,432]{0,1:T(8,128)(2,1)S(1)}, bf16[2560,432]{0,1:T(8,128)(2,1)}, u32[]{:S(2)}) copy-start(bf16[2560,432]{0,1:T(8,128)(2,1)} %param.25) | copy-start | bytes 6635524
  35.0 11.3 %copy-start.2 = (bf16[432,2560]{1,0:T(8,128)(2,1)S(1)}, bf16[432,2560]{1,0:T(8,128)(2,1)}, u32[]{:S(2)}) copy-start(bf16[432,2560]{1,0:T(8,128)(2,1)} %wd_ref.1) | copy-start | bytes 6635524
  35.0 11.3 %copy-start.14 = (bf16[2560]{0:T(1024)(128)(2,1)S(1)}, bf16[2560]{0:T(1024)(128)(2,1)}, u32[]{:S(2)}) copy-start(bf16[2560]{0:T(1024)(128)(2,1)} %gain_ref.3) | copy-start | bytes 15364
  46.2 15.3 %copy-start.8 = (bf16[8,4,320]{2,1,0:T(4,128)(2,1)S(1)}, bf16[8,4,320]{2,1,0:T(4,128)(2,1)}, u32[]{:S(2)}) copy-start(bf16[8,4,320]{2,1,0:T(4,128)(2,1)} %tokens_ref.3) | copy-start | bytes 61444

commit v6 on v5

--- a/solution.py
+++ b/solution.py
@@ -30,6 +30,7 @@
 SLOTS = WIN // NSEQ
 SSLOTS = 16
 HELD = SLOTS + 3 * SSLOTS
+WIDE = 384
 EPS = 1e-05
 MASKED = -1e30
 TP = ("y", "c")
@@ -155,7 +156,7 @@
 
     k_new = rope(mm(wk_ref[...], normed, NT)).T.astype(BF16)
     v_new = mm(wv_ref[...], normed, NT).astype(BF16)
-    q_t = mm(normed, wq_ref[...], NT).T
+    q_t = mm(wq_ref[...], normed, NT)
     q = jnp.concatenate([rope(q_t[h * HD : (h + 1) * HD]) for h in range(GROUP)], axis=1).astype(BF16)
 
     seen = hide_ref[...] == 0.0
@@ -170,23 +171,34 @@
     level = jnp.where(some, top + jnp.log(jnp.where(some, total, 1.0)), MASKED)
     filler = jnp.zeros((128 - HD - 3, GROUP * ROWS), F32)
     acc = jnp.concatenate([acc * (1.0 / jnp.where(some, total, 1.0)), *split3(level), filler], axis=0).T
+    heads = [acc[h * ROWS : (h + 1) * ROWS] for h in range(GROUP)]
+    packed = jnp.concatenate(
+        [v[:, :HD] for v in heads] + [v[:, HD : HD + 3] for v in heads] + [jnp.zeros((ROWS, WIDE - GROUP * (HD + 3)), F32)],
+        axis=1,
+    )
     for team in range(NG):
-        rows = jnp.concatenate(
-            [acc[h * ROWS + team * TOK : h * ROWS + (team + 1) * TOK] for h in range(GROUP)], axis=0
-        ).astype(BF16)
+        rows = packed[team * TOK : (team + 1) * TOK].astype(BF16)
         for to in range(NSEQ):
             if team_of(to) == team:
                 part_ref[to] = rows
 
 
 def combine_kernel(part_ref, wo_ref, out_ref):
-    part = part_ref[...]
-    src = iota((128, 128), 0)
-    spread = ((src >= HD) & (src < HD + 3)).astype(BF16)
-    level = mm(part.reshape(NSEQ * GROUP * TOK, 128), spread, NN).reshape(NSEQ, GROUP * TOK, 128)
-    factor = jnp.exp(level - jnp.max(level, axis=0, keepdims=True))
-    attended = jnp.sum(part.astype(F32) * factor, axis=0) / jnp.sum(factor, axis=0)
-    attended = jnp.concatenate([attended[h * TOK : (h + 1) * TOK, :HD] for h in range(GROUP)], axis=1)
+    part = part_ref[...].astype(F32).reshape(NSEQ * TOK, WIDE)
+    src = iota((WIDE, WIDE), 0) - GROUP * HD
+    dst = iota((WIDE, WIDE), 1)
+    spread = jnp.zeros((WIDE, WIDE), F32)
+    for h in range(GROUP):
+        at_head = (dst >= h * HD) & (dst < (h + 1) * HD) & (src >= 3 * h) & (src < 3 * h + 3)
+        spread = jnp.where(at_head, 1.0, spread)
+    level = mm(part.astype(BF16), spread.astype(BF16), NN).reshape(NSEQ * TOK // 8, 8, WIDE)
+    top = jnp.max(level, axis=0)
+    top = jnp.maximum(top, pltpu.roll(top, TOK, 0))
+    factor = jnp.exp(level - top)
+    weighted = jnp.sum(part.reshape(NSEQ * TOK // 8, 8, WIDE) * factor, axis=0)
+    total = jnp.sum(factor, axis=0)
+    attended = (weighted + pltpu.roll(weighted, TOK, 0)) / (total + pltpu.roll(total, TOK, 0))
+    attended = attended[:TOK, : GROUP * HD]
     term = mm(attended.astype(BF16), wo_ref[...], NN).astype(BF16)
     for to in range(NTP):
         out_ref[to] = term
@@ -253,7 +265,7 @@
     x_all = lax.all_to_all(copies, TP, 0, 0, tiled=True)
     parts, own = call(
         attend_kernel,
-        (jax.ShapeDtypeStruct((NSEQ, GROUP * TOK, 128), BF16), jax.ShapeDtypeStruct((TOK, D), F32)),
+        (jax.ShapeDtypeStruct((NSEQ, TOK, WIDE), BF16), jax.ShapeDtypeStruct((TOK, D), F32)),
         (
             x_all, attn_gain, *tables, proj_query.T, proj_key.T, proj_value.T,
         ),

time: 62.6 us -> 62.3 us (level)
  no operation moved by 1% of the time
where the time goes in v6:
time: 62.3 us; the launch traced here: 62 us
  blocking collectives  43.5 us (70%)
  starting transfers between devices  6.48 us (10%)
  Pallas kernels  6.32 us (10%)
  waiting for transfers between devices  4.08 us (7%)
  between operations  0.84 us (1%)
  local copies, waits for them, and re-layouts  0.82 us (1%)
    all_to_all x1, blocking collectives, body(): parts = lax.all_to_all(parts, SEQ, 0, 0, tiled=True)  19.4 us
    all_to_all x1, blocking collectives, body(): pieces = lax.all_to_all(pieces, TEAM + TP, 0, 0, tiled=True)  13.6 us
    all_to_all x1, blocking collectives, body(): terms = lax.all_to_all(terms, TP, 0, 0, tiled=True)  10.5 us
    all_to_all x1, starting transfers between devices, body(): x_all = lax.all_to_all(copies, TP, 0, 0, tiled=True)  6.48 us
    pallas_call x6, Pallas kernels, call(): pl.pallas_call(kernel, out_shape=out_shape, in_specs=specs, scratch_shape...  6.32 us
    all_to_all x1, waiting for transfers between devices, body(): x_all = lax.all_to_all(copies, TP, 0, 0, tiled=True)  4.08 us
  transfers between devices with their start and end apart: 1, of which 1 were waited for; matrix products, arithmetic and copies ran while one was open for 0% of the time, Pallas kernels for 1%

profile of v6, /device:TPU:1, one launch (start us, length us, event | category | flops | bytes accessed | tf_op | source)
XLA Modules:
  0.0 62.0 jit_solution(1629046861483492006)
XLA Ops:
  0.0 0.7 %copy-done.7 = bf16[8,4,320]{2,1,0:T(4,128)(2,1)S(1)} copy-done((bf16[8,4,320]{2,1,0:T(4,128)(2,1)S(1)}, bf16[8,4,320]{2,1,0:T(4,128)(2,1)}, u32[]{:S(2)}) %copy-start.7) | copy-done | bytes 20504
  0.7 0.0 copy-start.15
  0.8 0.0 copy-start.16
  0.8 0.7 %shard_map.163 = (bf16[8,80,128]{2,1,0:T(8,128)(2,1)}, f32[8,128]{1,0:T(8,128)S(1)}) custom-call(bf16[8,4,320]{2,1,0:T(4,128)(2,1)S(1)} %copy-done.7), custom_call_target="tpu_custom_call" | custom-call | flops 49999998976 | bytes 100000000 | tf_op jit(solution)/shard_map/pallas_call | solution.py:230
  1.5 6.5 %all-to-all-start = ((bf16[8,80,128]{2,1,0:T(8,128)(2,1)}), bf16[8,80,128]{2,1,0:T(8,128)(2,1)S(1)}, u32[]{:S(2)}, u32[]{:S(2)}) async-start(bf16[8,80,128]{2,1,0:T(8,128)(2,1)} %get-tuple-element.14), calls=%async_computation | async-start | bytes 327680 | tf_op jit(solution)/shard_map/all_to_all | solution.py:265
  8.6 0.0 copy-done.9
  8.7 0.0 copy-done.10
  8.7 0.0 copy-done.11
  8.7 0.0 copy-done.12
  8.7 0.0 copy-done.15
  8.7 0.0 copy-done.16
  8.7 0.0 copy-start.3
  8.7 0.0 copy-start.5
  8.7 0.0 copy-start.6
  8.7 0.0 copy-start.13
  8.8 0.7 %shard_map.164 = (f32[40,32]{1,0:T(8,128)S(1)}, f32[40,32]{1,0:T(8,128)S(1)}, f32[208,128]{1,0:T(8,128)S(1)}, bf16[176,80]{1,0:T(8,128)(2,1)S(1)}, bf16[80,176]{1,0:T(8,128)(2,1)S(1)}) custom-call(f32[8,128]{1,0:T(8,128)S(1)} %get-tuple-element.15.after_ref, s32[1]{0:T(128)S(6)} %copy.18.seen_hbm, s32[3]{0:T(128)S(1)} %copy-done.15, ...), custom_call_target="tpu_custom_call" | custom-call | flops 49999998976 | bytes 100000000 | tf_op jit(solution)/shard_map/pallas_call | solution.py:230
  9.5 4.1 %all-to-all-done.x_ref = bf16[8,80,128]{2,1,0:T(8,128)(2,1)S(1)} async-done(((bf16[8,80,128]{2,1,0:T(8,128)(2,1)}), bf16[8,80,128]{2,1,0:T(8,128)(2,1)S(1)}, u32[]{:S(2)}, u32[]{:S(2)}) %all-to-all-start) | async-done | bytes 163872 | tf_op jit(solution)/shard_map/all_to_all | solution.py:265
  13.6 0.0 copy-done.3
  13.6 0.0 copy-done.5
  13.6 0.0 copy-done.6
  13.6 0.0 copy-done.13
  13.6 0.0 copy-start.4
  13.6 1.7 %shard_map.165 = (bf16[32,4,384]{2,1,0:T(4,128)(2,1)S(1)}, f32[4,2560]{1,0:T(4,128)S(1)}) custom-call(bf16[8,80,128]{2,1,0:T(8,128)(2,1)S(1)} %all-to-all-done.x_ref, bf16[2560]{0:T(1024)(128)(2,1)S(1)} %copy-done.13, f32[40,32]{1,0:T(8,128)S(1)} %get-tuple-element.16.cos_ref, f32[40,32]{1,0:T(8,128)S(1)} %get-tuple-element.17.sin_ref, ...), custom_call_target="tpu_custom_call" | custom-call | flops 49999998976 | bytes 100000000 | tf_op jit(solution)/shard_map/pallas_call | solution.py:230
  15.3 19.4 %all_to_all.20.part_ref = bf16[32,4,384]{2,1,0:T(4,128)(2,1)S(1)} all-to-all(bf16[32,4,384]{2,1,0:T(4,128)(2,1)S(1)} %get-tuple-element.21), channel_id=1, replica_groups=mesh['zh'=4,'zl'=2,'xh'=2,'xl'=2,'y'=4,'c'=2] {'zh','zl','xh','xl'}, dimensions={0} | all-to-all | bytes 196608 | tf_op jit(solution)/shard_map/all_to_all | solution.py:273
  34.7 0.0 copy-start.14
  34.7 0.6 shard_map.166
  35.3 10.5 %all_to_all.21.part_ref = bf16[8,4,2560]{2,1,0:T(4,128)(2,1)S(1)} all-to-all(bf16[8,4,2560]{2,1,0:T(4,128)(2,1)S(1)} %shard_map.166), channel_id=1, replica_groups=mesh['zh'=4,'zl'=2,'xh'=2,'xl'=2,'y'=4,'c'=2] {'y','c'}, dimensions={0} | all-to-all | bytes 327680 | tf_op jit(solution)/shard_map/all_to_all | solution.py:275
  45.8 0.0 copy-done.1
  45.8 0.0 copy-start.8
  45.8 1.8 %shard_map.167 = bf16[64,5,2,128]{3,2,1,0:T(2,128)(2,1)S(1)} custom-call(bf16[8,4,2560]{2,1,0:T(4,128)(2,1)S(1)} %all_to_all.21.part_ref, f32[4,2560]{1,0:T(4,128)S(1)} %get-tuple-element.22.own_ref, bf16[2560]{0:T(1024)(128)(2,1)S(1)} %copy-done.14, bf16[432,2560]{1,0:T(8,128)(2,1)S(1)} %bitcast.13, bf16[432,2560]{1,0:T(8,128)(2,1)S(1)} %bitcast.14, ...), custom_call_target="tpu_custom_call" | custom-call | flops 49999998976 | bytes 100000000 | tf_op jit(solution)/shard_map/pallas_call | solution.py:230
  47.7 13.6 %all_to_all.22.piece_ref = bf16[64,5,2,128]{3,2,1,0:T(2,128)(2,1)S(1)} all-to-all(bf16[64,5,2,128]{3,2,1,0:T(2,128)(2,1)S(1)} %shard_map.167), channel_id=1, replica_groups=mesh['zh'=4,'zl'=2,'xh'=2,'xl'=2,'y'=4,'c'=2] {'zl','xh','xl','y','c'}, dimensions={0} | all-to-all | bytes 327680 | tf_op jit(solution)/shard_map/all_to_all | solution.py:281
  61.3 0.8 %shard_map.168 = bf16[8,4,320]{2,1,0:T(4,128)(2,1)} custom-call(bf16[64,5,2,128]{3,2,1,0:T(2,128)(2,1)S(1)} %all_to_all.22.piece_ref, bf16[8,4,320]{2,1,0:T(4,128)(2,1)S(1)} %copy-done.8), custom_call_target="tpu_custom_call" | custom-call | flops 49999998976 | bytes 100000000 | tf_op jit(solution)/shard_map/pallas_call | solution.py:230
  (13 shorter events, 0.0 us)
Async XLA Ops:
  0.0 0.7 %copy-start.7 = (bf16[8,4,320]{2,1,0:T(4,128)(2,1)S(1)}, bf16[8,4,320]{2,1,0:T(4,128)(2,1)}, u32[]{:S(2)}) copy-start(bf16[8,4,320]{2,1,0:T(4,128)(2,1)} %tokens_ref.3) | copy-start | bytes 61444
  0.7 7.9 %copy-start.9 = (bf16[128,1,80]{0,2,1:T(8,128)(2,1)S(1)}, bf16[128,1,80]{0,2,1:T(8,128)(2,1)}, u32[]{:S(2)}) copy-start(bf16[128,1,80]{0,2,1:T(8,128)(2,1)} %param.27) | copy-start | bytes 61444
  0.7 7.9 %copy-start.10 = (bf16[128,1,80]{0,2,1:T(8,128)(2,1)S(1)}, bf16[128,1,80]{0,2,1:T(8,128)(2,1)}, u32[]{:S(2)}) copy-start(bf16[128,1,80]{0,2,1:T(8,128)(2,1)} %param.28) | copy-start | bytes 61444
  0.7 7.9 %copy-start.11 = (bf16[16,1,240]{2,0,1:T(8,128)(2,1)S(1)}, bf16[16,1,240]{2,0,1:T(8,128)(2,1)}, u32[]{:S(2)}) copy-start(bf16[16,1,240]{2,0,1:T(8,128)(2,1)} %param.29) | copy-start | bytes 23044
  0.7 7.9 %copy-start.12 = (bf16[16,1,240]{2,0,1:T(8,128)(2,1)S(1)}, bf16[16,1,240]{2,0,1:T(8,128)(2,1)}, u32[]{:S(2)}) copy-start(bf16[16,1,240]{2,0,1:T(8,128)(2,1)} %param.30) | copy-start | bytes 23044
  0.7 7.9 %copy-start.15 = (s32[3]{0:T(128)S(1)}, s32[3]{0:T(128)}, u32[]{:S(2)}) copy-start(s32[3]{0:T(128)} %len_hbm.1) | copy-start | bytes 40
  0.8 7.9 %copy-start.16 = (f32[40,32]{1,0:T(8,128)S(1)}, f32[40,32]{1,0:T(8,128)}, u32[]{:S(2)}) copy-start(f32[40,32]{1,0:T(8,128)} %constant.2.clone.freq_ref) | copy-start | bytes 15364
  1.5 12.1 %all-to-all-start = ((bf16[8,80,128]{2,1,0:T(8,128)(2,1)}), bf16[8,80,128]{2,1,0:T(8,128)(2,1)S(1)}, u32[]{:S(2)}, u32[]{:S(2)}) async-start(bf16[8,80,128]{2,1,0:T(8,128)(2,1)} %get-tuple-element.14), calls=%async_computation | async-start | bytes 327680 | tf_op jit(solution)/shard_map/all_to_all | solution.py:265
  8.7 4.9 %copy-start.3 = (bf16[2560,320]{0,1:T(8,128)(2,1)S(1)}, bf16[2560,320]{0,1:T(8,128)(2,1)}, u32[]{:S(2)}) copy-start(bf16[2560,320]{0,1:T(8,128)(2,1)} %param.20) | copy-start | bytes 4915204
  8.7 4.9 %copy-start.5 = (bf16[2560,80]{0,1:T(8,128)(2,1)S(1)}, bf16[2560,80]{0,1:T(8,128)(2,1)}, u32[]{:S(2)}) copy-start(bf16[2560,80]{0,1:T(8,128)(2,1)} %param.21) | copy-start | bytes 1228804
  8.7 4.8 %copy-start.6 = (bf16[2560,80]{0,1:T(8,128)(2,1)S(1)}, bf16[2560,80]{0,1:T(8,128)(2,1)}, u32[]{:S(2)}) copy-start(bf16[2560,80]{0,1:T(8,128)(2,1)} %param.22) | copy-start | bytes 1228804
  8.7 4.8 %copy-start.13 = (bf16[2560]{0:T(1024)(128)(2,1)S(1)}, bf16[2560]{0:T(1024)(128)(2,1)}, u32[]{:S(2)}) copy-start(bf16[2560]{0:T(1024)(128)(2,1)} %gain_ref.2) | copy-start | bytes 15364
  13.6 21.1 %copy-start.4 = (bf16[320,2560]{1,0:T(8,128)(2,1)S(1)}, bf16[320,2560]{1,0:T(8,128)(2,1)}, u32[]{:S(2)}) copy-start(bf16[320,2560]{1,0:T(8,128)(2,1)} %wo_ref.1) | copy-start | bytes 4915204
  34.6 11.2 %copy-start = (bf16[2560,432]{0,1:T(8,128)(2,1)S(1)}, bf16[2560,432]{0,1:T(8,128)(2,1)}, u32[]{:S(2)}) copy-start(bf16[2560,432]{0,1:T(8,128)(2,1)} %param.24) | copy-start | bytes 6635524
  34.7 11.2 %copy-start.1 = (bf16[2560,432]{0,1:T(8,128)(2,1)S(1)}, bf16[2560,432]{0,1:T(8,128)(2,1)}, u32[]{:S(2)}) copy-start(bf16[2560,432]{0,1:T(8,128)(2,1)} %param.25) | copy-start | bytes 6635524
  34.7 11.2 %copy-start.2 = (bf16[432,2560]{1,0:T(8,128)(2,1)S(1)}, bf16[432,2560]{1,0:T(8,128)(2,1)}, u32[]{:S(2)}) copy-start(bf16[432,2560]{1,0:T(8,128)(2,1)} %wd_ref.1) | copy-start | bytes 6635524
  34.7 11.2 %copy-start.14 = (bf16[2560]{0:T(1024)(128)(2,1)S(1)}, bf16[2560]{0:T(1024)(128)(2,1)}, u32[]{:S(2)}) copy-start(bf16[2560]{0:T(1024)(128)(2,1)} %gain_ref.3) | copy-start | bytes 15364
  45.8 15.4 %copy-start.8 = (bf16[8,4,320]{2,1,0:T(4,128)(2,1)S(1)}, bf16[8,4,320]{2,1,0:T(4,128)(2,1)}, u32[]{:S(2)}) copy-start(bf16[8,4,320]{2,1,0:T(4,128)(2,1)} %tokens_ref.3) | copy-start | bytes 61444
